TPU v7x, 32 devices: a whole 2x2x4 slice. The times are simulated.
32 devices in a mesh: fsdp: 8 (over y, x, core), rep: 4 (over z).
Axes of the slice: x: 2, y: 2, z: 4, core: 2. Of those that a mesh axis runs over, the one named last changes fastest.
Arguments:
- layer_input: bfloat16 [128, 512, 768], P(('fsdp', 'rep')), may hold values from -6 to 6
- segment_length_pairs: int32 [128, 2], P(('fsdp', 'rep')), may hold values from 16 to 496, as said below
- query_key_value_weight: bfloat16 [3, 768, 768], P(None, 'fsdp', 'rep'), may hold values from -0.21875 to 0.21875
- output_weight: bfloat16 [768, 768], P('fsdp', 'rep'), may hold values from -0.875 to 0.875
- attention_bias: bfloat16 [3, 768], P(None, 'fsdp'), may hold values from -1.5 to 1.5
- adapter_down: bfloat16 [2, 768, 8], P(None, 'fsdp'), may hold values from -0.21875 to 0.21875
- adapter_up: bfloat16 [2, 8, 768], replicated, may hold values from -1 to 1
- layernorm_gain: bfloat16 [2, 768], P(None, 'fsdp'), may hold values from 0.5 to 1.5
- layernorm_bias: bfloat16 [2, 768], P(None, 'fsdp'), may hold values from -1.5 to 1.5
- feedforward_in_weight: bfloat16 [768, 3072], P('fsdp', 'rep'), may hold values from -0.21875 to 0.21875
- feedforward_in_bias: bfloat16 [3072], P('fsdp'), may hold values from -1.5 to 1.5
- feedforward_out_weight: bfloat16 [3072, 768], P('fsdp', 'rep'), may hold values from -0.21875 to 0.21875
- feedforward_out_bias: bfloat16 [768], P('fsdp'), may hold values from -1.5 to 1.5
- output_cotangent: bfloat16 [128, 512, 768], P(('fsdp', 'rep')), may hold values from -6 to 6
Outputs:
- hidden_out: bfloat16 [128, 512, 768], P(('fsdp', 'rep'))
- hidden_grad: bfloat16 [128, 512, 768], P(('fsdp', 'rep'))
- adapter_up_gradient: float32 [2, 8, 768], replicated
Inputs may be any that keep to these rules, and one draw needn't show every extreme that they name: Item i uses slots 0 to segment_length_pairs[i,0] + segment_length_pairs[i,1] - 1 of its 512; that total is at most 512, and exactly 512 for every item whose index is a multiple of 4. The first segment is at most 256. Item 0 has a first segment of 16 and a second of 496; item 1 has a second segment of 16.
All inputs are finite; a program needn't handle non-finite values.
Results may differ from a plain program's by a relative error of at most 0.017.
Values may be sent and summed in bfloat16 or wider, within the bound.
No kernel may reach another device: no remote copies, remote signals or barrier semaphores. Data moves between devices by JAX's collectives and lax.ppermute only.
A program may use at most 320 MiB of HBM per device.

v0:
```python
import math
import jax
import jax.numpy as jnp
from jax import lax
from jax.sharding import PartitionSpec as P

MODEL_WIDTH = 768
H = 12
HD = 64
ADAPTER_RANK = 8
ADAPTER_ALPHA = 16
L = 512
MB = 2


def collect_frozen(frozen_args):
    (
        qkv_part,
        out_part,
        in_part,
        back_part,
        attn_part,
        down_part,
        gain_part,
        shift_part,
        in_bias_part,
        back_bias_part,
    ) = frozen_args
    columns = (
        lax.all_gather(qkv_part, "rep", axis=2, tiled=True),
        lax.all_gather(out_part, "rep", axis=1, tiled=True),
        lax.all_gather(in_part, "rep", axis=1, tiled=True),
        lax.all_gather(back_part, "rep", axis=1, tiled=True),
    )
    return (
        lax.all_gather(columns[0], "fsdp", axis=1, tiled=True),
        lax.all_gather(columns[1], "fsdp", axis=0, tiled=True),
        lax.all_gather(columns[2], "fsdp", axis=0, tiled=True),
        lax.all_gather(columns[3], "fsdp", axis=0, tiled=True),
        lax.all_gather(attn_part, "fsdp", axis=1, tiled=True),
        lax.all_gather(down_part, "fsdp", axis=1, tiled=True),
        lax.all_gather(gain_part, "fsdp", axis=1, tiled=True),
        lax.all_gather(shift_part, "fsdp", axis=1, tiled=True),
        lax.all_gather(in_bias_part, "fsdp", axis=0, tiled=True),
        lax.all_gather(back_bias_part, "fsdp", axis=0, tiled=True),
    )


def adapter_sum(adapter_grad_term):
    return lax.psum(adapter_grad_term, ("fsdp", "rep"))


def exact_gelu(values):
    return jax.nn.gelu(values, approximate=False)


def layer_norm_rows(values):
    centered = values - jnp.mean(values, axis=-1, keepdims=True)
    spread = jnp.mean(centered * centered, axis=-1, keepdims=True)
    inverse = lax.rsqrt(spread + 1e-05)
    return (centered * inverse, inverse)


def norm_back(output_gradient, normed, inverse, gain):
    scaled = output_gradient * gain
    return inverse * (
        scaled
        - jnp.mean(scaled, axis=-1, keepdims=True)
        - normed * jnp.mean(scaled * normed, axis=-1, keepdims=True)
    )


def attention_scores(query_bf, key_bf, valid_keys):
    head_scale = 1.0 / math.sqrt(HD)
    raw_scores = (
        jnp.einsum("ilhe,imhe->ihlm", query_bf, key_bf, preferred_element_type=jnp.float32)
        * head_scale
    )
    return jnp.where(valid_keys[:, None, None, :], raw_scores, -1e30)


def forward_sweep(input_bundle, valid_keys, weight_bundle, adapter_up):
    (
        qkv_full,
        out_full,
        in_full,
        back_full,
        attention_offset,
        down_matrix_whole,
        norm_gains,
        norm_shifts,
        in_shift,
        back_shift,
    ) = weight_bundle
    item_count = valid_keys.shape[0]
    row_count = input_bundle.shape[0]
    adapter_scale = ADAPTER_ALPHA / ADAPTER_RANK
    attention_single = attention_offset.astype(jnp.float32)
    adapter_reduced = jnp.einsum(
        "td,kdr->tkr", input_bundle, down_matrix_whole, preferred_element_type=jnp.float32
    ).astype(jnp.bfloat16)
    projected_rows = jnp.einsum(
        "td,kde->tke", input_bundle, qkv_full, preferred_element_type=jnp.float32
    )
    adapter_term = jnp.einsum(
        "lsn,snb->lsb", adapter_reduced, adapter_up, preferred_element_type=jnp.float32
    )
    head_shape = (item_count, L, H, HD)
    query_bf = (
        (projected_rows[:, 0] + attention_single[0] + adapter_scale * adapter_term[:, 0])
        .astype(jnp.bfloat16)
        .reshape(head_shape)
    )
    key_bf = projected_rows[:, 1].astype(jnp.bfloat16).reshape(head_shape)
    value_bf = (
        (projected_rows[:, 2] + attention_single[1] + adapter_scale * adapter_term[:, 1])
        .astype(jnp.bfloat16)
        .reshape(head_shape)
    )
    scores = attention_scores(query_bf, key_bf, valid_keys)
    row_max = jnp.max(scores, axis=-1, keepdims=True)
    log_total = row_max + jnp.log(jnp.sum(jnp.exp(scores - row_max), axis=-1, keepdims=True))
    probs_bf = jnp.exp(scores - log_total).astype(jnp.bfloat16)
    mixed_bf = (
        jnp.einsum("ihlm,imhe->ilhe", probs_bf, value_bf, preferred_element_type=jnp.float32)
        .astype(jnp.bfloat16)
        .reshape(row_count, MODEL_WIDTH)
    )
    first_sum = (
        input_bundle.astype(jnp.float32)
        + jnp.dot(mixed_bf, out_full, preferred_element_type=jnp.float32)
        + attention_single[2]
    )
    normed_one, inverse_one = layer_norm_rows(first_sum)
    gain_float = norm_gains.astype(jnp.float32)
    shift_float = norm_shifts.astype(jnp.float32)
    hidden_one = normed_one * gain_float[0] + shift_float[0]
    ffn_inner = jnp.dot(
        hidden_one.astype(jnp.bfloat16), in_full, preferred_element_type=jnp.float32
    ) + in_shift.astype(jnp.float32)
    activation = exact_gelu(ffn_inner).astype(jnp.bfloat16)
    second_sum = (
        hidden_one
        + jnp.dot(activation, back_full, preferred_element_type=jnp.float32)
        + back_shift.astype(jnp.float32)
    )
    normed_two, inverse_two = layer_norm_rows(second_sum)
    layer_output = (normed_two * gain_float[1] + shift_float[1]).astype(jnp.bfloat16)
    saved_values = (
        adapter_reduced,
        query_bf,
        key_bf,
        value_bf,
        log_total,
        normed_one,
        inverse_one,
        ffn_inner,
        normed_two,
        inverse_two,
    )
    return (saved_values, layer_output)


def reverse_sweep(output_gradient, saved_values, valid_keys, weight_bundle, adapter_up):
    (
        qkv_full,
        out_full,
        in_full,
        back_full,
        attention_offset,
        down_matrix_whole,
        norm_gains,
        norm_shifts,
        in_shift,
        back_shift,
    ) = weight_bundle
    (
        adapter_reduced,
        query_bf,
        key_bf,
        value_bf,
        log_total,
        normed_one,
        inverse_one,
        ffn_inner,
        normed_two,
        inverse_two,
    ) = saved_values
    item_count = valid_keys.shape[0]
    row_count = output_gradient.shape[0]
    adapter_scale = ADAPTER_ALPHA / ADAPTER_RANK
    head_scale = 1.0 / math.sqrt(HD)
    gain_float = norm_gains.astype(jnp.float32)
    grad_second = norm_back(
        output_gradient.astype(jnp.float32), normed_two, inverse_two, gain_float[1]
    )
    grad_act = jnp.einsum(
        "td,fd->tf", grad_second.astype(jnp.bfloat16), back_full, preferred_element_type=jnp.float32
    )
    gelu_value, gelu_pull = jax.vjp(exact_gelu, ffn_inner)
    grad_inner = gelu_pull(grad_act)[0].astype(jnp.bfloat16)
    grad_hidden = grad_second + jnp.einsum(
        "tf,df->td", grad_inner, in_full, preferred_element_type=jnp.float32
    )
    grad_first = norm_back(grad_hidden, normed_one, inverse_one, gain_float[0])
    grad_mixed = jnp.einsum(
        "td,ed->te", grad_first.astype(jnp.bfloat16), out_full, preferred_element_type=jnp.float32
    )
    grad_mixed = grad_mixed.astype(jnp.bfloat16).reshape(item_count, L, H, HD)
    scores = attention_scores(query_bf, key_bf, valid_keys)
    attn_weights = jnp.exp(scores - log_total)
    probs_bf = attn_weights.astype(jnp.bfloat16)
    grad_probs = jnp.einsum(
        "ilhe,imhe->ihlm", grad_mixed, value_bf, preferred_element_type=jnp.float32
    )
    value_gradient = jnp.einsum(
        "ihlm,ilhe->imhe", probs_bf, grad_mixed, preferred_element_type=jnp.float32
    ).astype(jnp.bfloat16)
    row_inner = jnp.sum(attn_weights * grad_probs, axis=-1, keepdims=True)
    grad_scores = (attn_weights * (grad_probs - row_inner)).astype(jnp.bfloat16)
    query_gradient = (
        jnp.einsum("ihlm,imhe->ilhe", grad_scores, key_bf, preferred_element_type=jnp.float32)
        * head_scale
    ).astype(jnp.bfloat16)
    grad_key = (
        jnp.einsum("ihlm,ilhe->imhe", grad_scores, query_bf, preferred_element_type=jnp.float32)
        * head_scale
    ).astype(jnp.bfloat16)
    query_gradient = query_gradient.reshape(row_count, MODEL_WIDTH)
    grad_key = grad_key.reshape(row_count, MODEL_WIDTH)
    value_gradient = value_gradient.reshape(row_count, MODEL_WIDTH)
    grad_proj = jnp.stack([query_gradient, grad_key, value_gradient], axis=1)
    input_gradient = grad_first + jnp.einsum(
        "tke,kde->td", grad_proj, qkv_full, preferred_element_type=jnp.float32
    )
    adapter_gradient = jnp.stack([query_gradient, value_gradient], axis=1)
    adapter_grad_term = adapter_scale * jnp.einsum(
        "hiu,his->ius", adapter_reduced, adapter_gradient, preferred_element_type=jnp.float32
    )
    grad_u = (
        adapter_scale
        * jnp.einsum(
            "pqf,qnf->pqn", adapter_gradient, adapter_up, preferred_element_type=jnp.float32
        )
    ).astype(jnp.bfloat16)
    input_gradient = input_gradient + jnp.einsum(
        "tkr,kdr->td", grad_u, down_matrix_whole, preferred_element_type=jnp.float32
    )
    return (input_gradient.astype(jnp.bfloat16), adapter_grad_term)


def per_device(
    layer_input,
    segment_length_pairs,
    query_key_value_weight,
    output_weight,
    attention_bias,
    adapter_down,
    adapter_up,
    layernorm_gain,
    layernorm_bias,
    feedforward_in_weight,
    feedforward_in_bias,
    feedforward_out_weight,
    feedforward_out_bias,
    output_cotangent,
):
    frozen_args = (
        query_key_value_weight,
        output_weight,
        feedforward_in_weight,
        feedforward_out_weight,
        attention_bias,
        adapter_down,
        layernorm_gain,
        layernorm_bias,
        feedforward_in_bias,
        feedforward_out_bias,
    )
    per_micro = layer_input.shape[0] // MB
    row_count = per_micro * L
    token_count = layer_input.shape[0] * L * lax.axis_size("fsdp") * lax.axis_size("rep")
    positions = jnp.arange(L, dtype=jnp.int32)
    layer_outputs = []
    input_gradients = []
    gradient_total = jnp.zeros((2, ADAPTER_RANK, MODEL_WIDTH), jnp.float32)
    for micro_index in range(MB):
        weight_bundle = collect_frozen(frozen_args)
        first_item = micro_index * per_micro
        input_bundle = layer_input[first_item : first_item + per_micro].reshape(
            row_count, MODEL_WIDTH
        )
        valid_counts = (
            segment_length_pairs[first_item : first_item + per_micro, 0]
            + segment_length_pairs[first_item : first_item + per_micro, 1]
        )
        valid_keys = positions[None, :] < valid_counts[:, None]
        saved_values, layer_output = forward_sweep(
            input_bundle, valid_keys, weight_bundle, adapter_up
        )
        weight_bundle = collect_frozen(frozen_args)
        gradient_rows = output_cotangent[first_item : first_item + per_micro].reshape(
            row_count, MODEL_WIDTH
        )
        input_gradient, adapter_grad_term = reverse_sweep(
            gradient_rows, saved_values, valid_keys, weight_bundle, adapter_up
        )
        gradient_total = gradient_total + adapter_grad_term
        layer_outputs.append(layer_output.reshape(per_micro, L, MODEL_WIDTH))
        input_gradients.append(input_gradient.reshape(per_micro, L, MODEL_WIDTH))
    gradient_total = adapter_sum(gradient_total)
    adapter_up_gradient = gradient_total / math.sqrt(token_count)
    return (
        jnp.concatenate(layer_outputs, axis=0),
        jnp.concatenate(input_gradients, axis=0),
        adapter_up_gradient,
    )


def solution(mesh):
    in_specs = (
        P(("fsdp", "rep"), None, None),
        P(("fsdp", "rep"), None),
        P(None, "fsdp", "rep"),
        P("fsdp", "rep"),
        P(None, "fsdp"),
        P(None, "fsdp", None),
        P(),
        P(None, "fsdp"),
        P(None, "fsdp"),
        P("fsdp", "rep"),
        P("fsdp"),
        P("fsdp", "rep"),
        P("fsdp"),
        P(("fsdp", "rep"), None, None),
    )
    out_specs = (P(("fsdp", "rep"), None, None), P(("fsdp", "rep"), None, None), P())
    return jax.shard_map(
        per_device, mesh=mesh, in_specs=in_specs, out_specs=out_specs, check_vma=False
    )
```

profile of v0, /device:TPU:0, one launch (start us, length us, event | category | flops | bytes accessed | tf_op | source)
XLA Modules:
  0.0 779.1 jit_solution(15271656868781157294)
XLA Ops:
  8.4 21.9 %all_gather.28 = bf16[3,96,768]{1,0,2:T(4,128)(2,1)} all-gather(bf16[3,96,192]{1,0,2:T(4,128)(2,1)S(1)} %copy.229), channel_id=1, replica_groups=mesh['fsdp'=8,'rep'=4] {'rep'}, dimensions={2}, use_global_device_ids=true | all-gather | bytes 552960 | tf_op jit(solution)/shard_map/all_gather | solution.py:30
  33.4 13.6 %all_gather.32 = bf16[96,768]{0,1:T(8,128)(2,1)S(1)} all-gather(bf16[96,192]{0,1:T(8,128)(2,1)S(1)} %copy.244), channel_id=1, replica_groups=mesh['fsdp'=8,'rep'=4] {'rep'}, dimensions={1}, use_global_device_ids=true | all-gather | bytes 184320 | tf_op jit(solution)/shard_map/all_gather | solution.py:31
  47.8 17.4 %all_gather.36 = bf16[96,3072]{1,0:T(8,128)(2,1)} all-gather(bf16[96,768]{1,0:T(8,128)(2,1)} %param.23), channel_id=1, replica_groups=mesh['fsdp'=8,'rep'=4] {'rep'}, dimensions={1}, use_global_device_ids=true | all-gather | bytes 737280 | tf_op jit(solution)/shard_map/all_gather | solution.py:32
  65.3 16.5 %all_gather.39 = bf16[384,768]{0,1:T(8,128)(2,1)} all-gather(bf16[384,192]{0,1:T(8,128)(2,1)} %param.25), channel_id=1, replica_groups=mesh['fsdp'=8,'rep'=4] {'rep'}, dimensions={1}, use_global_device_ids=true | all-gather | bytes 737280 | tf_op jit(solution)/shard_map/all_gather | solution.py:33
  83.4 12.1 %all-reduce = bf16[768]{0:T(1024)(128)(2,1)S(1)} all-reduce(bf16[768]{0:T(1024)(128)(2,1)S(1)} %dynamic-update-slice), channel_id=1, replica_groups=mesh['fsdp'=8,'rep'=4] {'fsdp'}, use_global_device_ids=true, to_apply=%add | all-reduce | flops 768 | bytes 3072
  96.1 8.7 %all-gather.1 = bf16[8,96,2]{1,2,0:T(2,128)(2,1)S(1)} all-gather(bf16[1,96,2]{1,2,0:T(2,128)(2,1)S(1)} %bitcast.229), channel_id=1, replica_groups=mesh['fsdp'=8,'rep'=4] {'fsdp'}, dimensions={0}, use_global_device_ids=true | all-gather | bytes 3456 | tf_op jit(solution)/shard_map/all_gather | solution.py:42
  104.9 8.1 %all-gather.2 = bf16[8,96,2]{1,2,0:T(2,128)(2,1)S(1)} all-gather(bf16[1,96,2]{1,2,0:T(2,128)(2,1)S(1)} %bitcast.230), channel_id=1, replica_groups=mesh['fsdp'=8,'rep'=4] {'fsdp'}, dimensions={0}, use_global_device_ids=true | all-gather | bytes 3456 | tf_op jit(solution)/shard_map/all_gather | solution.py:43
  113.0 9.0 %all-gather = bf16[8,96,3]{1,2,0:T(4,128)(2,1)S(1)} all-gather(bf16[1,96,3]{1,2,0:T(4,128)(2,1)S(1)} %bitcast.228), channel_id=1, replica_groups=mesh['fsdp'=8,'rep'=4] {'fsdp'}, dimensions={0}, use_global_device_ids=true | all-gather | bytes 5184 | tf_op jit(solution)/shard_map/all_gather | solution.py:40
  124.8 8.2 %all-gather.3 = bf16[8,1,384]{2,1,0:T(2,128)(2,1)S(1)} all-gather(bf16[1,1,384]{2,1,0:T(2,128)(2,1)S(1)} %reshape.269), channel_id=1, replica_groups=mesh['fsdp'=8,'rep'=4] {'fsdp'}, dimensions={0}, use_global_device_ids=true | all-gather | bytes 6912 | tf_op jit(solution)/shard_map/all_gather | solution.py:44
  133.1 9.6 %all_gather.31 = bf16[2,768,8]{2,0,1:T(2,128)(2,1)S(1)} all-gather(bf16[2,96,8]{2,0,1:T(2,128)(2,1)S(1)} %copy.233), channel_id=1, replica_groups=mesh['fsdp'=8,'rep'=4] {'fsdp'}, dimensions={1}, use_global_device_ids=true | all-gather | bytes 27648 | tf_op jit(solution)/shard_map/all_gather | solution.py:41
  148.5 3.1 slice_multiply_fusion.2
  154.0 3.8 mul.313
  160.3 3.7 mul.311
  165.1 3.1 slice_multiply_fusion
  170.5 3.8 mul.333
  176.7 3.9 mul.331
  180.7 6.3 fusion.150
  188.3 3.6 fusion.143
  193.1 3.8 fusion.149
  198.2 3.1 fusion.142
  203.7 3.8 squeeze.11
  210.4 4.2 copy.248
  214.6 5.6 squeeze.10
  220.2 3.6 copy.236
  223.8 5.8 squeeze.9
  231.2 3.3 convert_element_type.205
  234.5 4.1 copy.231
  238.6 5.6 squeeze.8
  244.2 7.9 %add_convert_fusion.8 = (bf16[2,512,12,64]{1,0,3,2:T(2,128)(2,1)S(1)}, bf16[2,512,12,64]{1,0,3,2:T(2,128)(2,1)}) fusion(f32[2,512,12,64]{1,0,3,2:T(2,128)} %mul.313, f32[2,512,12,64]{1,0,3,2:T(2,128)} %squeeze.9, f32[12,64]{1,0:T(8,128)S(1)} %add.225, f32[2,512,12,64]{1,0,3,2:T(2,128)} %mul.333, f32[2,512,12,64]{1,0,3,2:T(2,128)} %squeeze.11), kind=kLoop, calls=%fused_computation.116 | loop fusion | flops 4718592 | bytes 15731712 | tf_op jit(solution)/shard_map/convert_element_type | solution.py:111
  252.1 11.1 %fusion = (f32[2,12,512]{2,1,0:T(8,128)S(1)}, f32[2,12,512,512]{2,3,1,0:T(8,128)}) fusion(pred[2,512]{1,0:T(4,128)(4,1)S(1)} %get-tuple-element.62, bf16[2,512,12,64]{1,0,3,2:T(2,128)(2,1)S(1)} %convert_element_type.205, bf16[2,512,12,64]{1,0,3,2:T(2,128)(2,1)S(1)} %get-tuple-element.36), kind=kOutput, calls=%fused_computation.10 | convolution fusion | flops 824168448 | bytes 28361728 | tf_op jit(solution)/shard_map/ilhe,imhe->ihlm/dot_general | solution.py:76
  263.2 12.8 %exponential_reduce_fusion.1 = f32[2,12,512]{2,1,0:T(8,128)S(1)} fusion(f32[2,12,512,512]{2,3,1,0:T(8,128)} %get-tuple-element.45, f32[2,12,512]{2,1,0:T(8,128)S(1)} %get-tuple-element.44, pred[2,512]{1,0:T(4,128)(4,1)S(1)} %get-tuple-element.62), kind=kLoop, calls=%fused_computation.8 | loop fusion | flops 25153536 | bytes 25265152 | tf_op jit(solution)/shard_map/reduce_sum | solution.py:122
  276.1 4.4 add_convert_fusion.9
  280.5 11.9 %fusion.66 = bf16[2,512,12,64]{1,3,2,0:T(8,128)(2,1)S(1)} fusion(bf16[2,512,12,64]{1,0,3,2:T(2,128)(2,1)S(1)} %get-tuple-element.38, f32[2,12,512,512]{2,3,1,0:T(8,128)} %get-tuple-element.45, f32[2,12,512]{2,1,0:T(8,128)S(1)} %log_add_fusion.1, pred[2,512]{1,0:T(4,128)(4,1)S(1)} %get-tuple-element.62), kind=kOutput, calls=%fused_computation.152 | convolution fusion | flops 831258624 | bytes 28361728 | tf_op jit(solution)/shard_map/ihlm,imhe->ilhe/dot_general | solution.py:125
  295.6 3.4 fusion.145
  301.6 11.1 %fusion.1 = (f32[2,12,512]{2,1,0:T(8,128)S(1)}, f32[2,12,512,512]{2,3,1,0:T(8,128)}) fusion(pred[2,512]{1,0:T(4,128)(4,1)S(1)} %get-tuple-element.61, bf16[2,512,12,64]{1,0,3,2:T(2,128)(2,1)S(1)} %convert_element_type.220, bf16[2,512,12,64]{1,0,3,2:T(2,128)(2,1)S(1)} %copy-done.7), kind=kOutput, calls=%fused_computation.11 | convolution fusion | flops 824168448 | bytes 28361728 | tf_op jit(solution)/shard_map/ilhe,imhe->ihlm/dot_general | solution.py:76
  312.7 11.2 %exponential_reduce_fusion = f32[2,12,512]{2,1,0:T(8,128)S(1)} fusion(f32[2,12,512,512]{2,3,1,0:T(8,128)} %get-tuple-element.43, f32[2,12,512]{2,1,0:T(8,128)S(1)} %get-tuple-element.42, pred[2,512]{1,0:T(4,128)(4,1)S(1)} %get-tuple-element.61), kind=kLoop, calls=%fused_computation.5 | loop fusion | flops 25153536 | bytes 25265152 | tf_op jit(solution)/shard_map/reduce_sum | solution.py:122
  324.0 11.6 %fusion.67 = bf16[2,512,12,64]{1,3,2,0:T(8,128)(2,1)S(1)} fusion(bf16[2,512,12,64]{1,0,3,2:T(2,128)(2,1)S(1)} %copy-done.29, f32[2,12,512,512]{2,3,1,0:T(8,128)} %get-tuple-element.43, f32[2,12,512]{2,1,0:T(8,128)S(1)} %log_add_fusion, pred[2,512]{1,0:T(4,128)(4,1)S(1)} %get-tuple-element.61), kind=kOutput, calls=%fused_computation.153 | convolution fusion | flops 831258624 | bytes 28361728 | tf_op jit(solution)/shard_map/ihlm,imhe->ilhe/dot_general | solution.py:125
  341.6 8.3 %fusion.48 = f32[1024,3072]{1,0:T(8,128)S(1)} fusion(bf16[768,3072]{1,0:T(8,128)(2,1)} %all-gather.13.cloned.1.call-done, f32[1024,768]{1,0:T(8,128)} %copy-done.38, f32[1024]{0:T(1024)S(1)} %add_rsqrt_fusion.1, f32[1024]{0:T(1024)S(1)} %broadcast_multiply_fusion.8, f32[768]{0:T(1024)S(1)} %get-tuple-element.17, f32[768]{0:T(1024)S(1)} %get-tuple-element.63), kind=kOutput, calls=%fused_computation.136 | convolution fusion | flops 4835770368 | bytes 20461568 | tf_op jit(solution)/shard_map/dot_general | solution.py:138
  349.9 4.5 copy-done.88
  354.5 59.2 %fusion.4 = (f32[1024,3072]{1,0:T(8,128)}, f32[1024,3072]{1,0:T(8,128)}, f32[1024,3072]{1,0:T(8,128)}) fusion(f32[3072]{0:T(1024)S(1)} %bitcast.223, f32[1024,3072]{1,0:T(8,128)S(1)} %fusion.48, bf16[768,3072]{1,0:T(8,128)(2,1)S(1)} %copy-done.81, f32[1024,768]{1,0:T(8,128)S(1)} %copy-done.35, f32[768]{0:T(1024)S(1)} %get-tuple-element.17, ...), kind=kOutput, calls=%fused_computation.16 | convolution fusion | flops 5232132096 | bytes 58222592 | tf_op jit(solution)/shard_map/dot_general | solution.py:138
  413.7 12.6 %fusion.147 = (f32[1024]{0:T(1024)S(1)}, f32[1024,768]{1,0:T(8,128)S(1)}) fusion(f32[768]{0:T(1024)S(1)} %copy-done.66, bf16[3072,768]{0,1:T(8,128)(2,1)} %all-gather.15.cloned.1.call-done, f32[1024,3072]{1,0:T(8,128)} %get-tuple-element.34, f32[1024,3072]{1,0:T(8,128)} %get-tuple-element.50, f32[3072]{0:T(1024)S(1)} %bitcast.224, ...), kind=kOutput, calls=%fused_computation.262 | convolution fusion | flops 4849925120 | bytes 36209664 | tf_op jit(solution)/shard_map/dot_general | solution.py:144
  427.0 16.0 %fusion.148 = (f32[1024]{0:T(1024)S(1)}, f32[1024,768]{1,0:T(8,128)S(1)}) fusion(f32[768]{0:T(1024)S(1)} %copy-done.66, bf16[3072,768]{0,1:T(8,128)(2,1)} %all-gather.15.cloned.1.call-done, f32[1024,3072]{1,0:T(8,128)} %get-tuple-element.35, f32[1024,3072]{1,0:T(8,128)} %copy-done.88, f32[3072]{0:T(1024)S(1)} %bitcast.225, f32[768]{0:T(1024)S(1)} %get-tuple-element.17, ...), kind=kOutput, calls=%fused_computation.263 | convolution fusion | flops 4849925120 | bytes 36209664 | tf_op jit(solution)/shard_map/dot_general | solution.py:144
  447.0 4.8 subtract_multiply_fusion.1
  451.9 22.1 %fusion.140 = (f32[1024]{0:T(1024)S(1)}, f32[1024]{0:T(1024)S(1)}, f32[1024,768]{1,0:T(8,128)}) fusion(f32[1024]{0:T(1024)S(1)} %add_rsqrt_fusion.3, f32[1024,768]{1,0:T(8,128)} %copy-done.34, f32[1024]{0:T(1024)S(1)} %broadcast_multiply_fusion.10, f32[768]{0:T(1024)S(1)} %get-tuple-element.63, f32[1024,768]{1,0:T(8,128)} %get-tuple-element.31, ...), kind=kOutput, calls=%fused_computation.255 | convolution fusion | flops 9717151744 | bytes 44071936 | tf_op jit(solution)/shard_map/tf,df->td/dot_general | solution.py:202
  474.6 5.3 convolution_convert_fusion.5
  482.9 12.8 %fusion.68 = bf16[2,512,12,64]{1,3,2,0:T(8,128)(2,1)} fusion(bf16[2,512,12,64]{1,0,3,2:T(2,128)(2,1)S(1)} %reshape.254, f32[2,12,512,512]{2,3,1,0:T(8,128)} %get-tuple-element.45, f32[2,12,512]{2,1,0:T(8,128)S(1)} %copy-done.48, pred[2,512]{1,0:T(4,128)(4,1)S(1)} %copy-done.56), kind=kOutput, calls=%fused_computation.154 | convolution fusion | flops 831258624 | bytes 28361728 | tf_op jit(solution)/shard_map/ihlm,ilhe->imhe/dot_general | solution.py:216
  495.7 19.7 %multiply_reduce_fusion.1 = (f32[2,12,512]{2,1,0:T(8,128)S(1)}, f32[2,12,512,512]{2,3,1,0:T(8,128)}) fusion(f32[2,12,512,512]{2,3,1,0:T(8,128)} %get-tuple-element.45, f32[2,12,512]{2,1,0:T(8,128)S(1)} %copy-done.48, pred[2,512]{1,0:T(4,128)(4,1)S(1)} %copy-done.56, bf16[2,512,12,64]{1,0,3,2:T(2,128)(2,1)S(1)} %copy-done.32, ...), kind=kOutput, calls=%fused_computation.3 | convolution fusion | flops 836751360 | bytes 53576704 | tf_op jit(solution)/shard_map/ilhe,imhe->ihlm/dot_general | solution.py:213
  515.4 21.6 %multiply_convert_fusion.1 = bf16[2,12,512,512]{2,3,1,0:T(8,128)(2,1)} fusion(f32[2,12,512,512]{2,3,1,0:T(8,128)} %get-tuple-element.60, f32[2,12,512,512]{2,3,1,0:T(8,128)} %get-tuple-element.45, f32[2,12,512]{2,1,0:T(8,128)S(1)} %get-tuple-element.59, f32[2,12,512]{2,1,0:T(8,128)S(1)} %copy-done.48, pred[2,512]{1,0:T(4,128)(4,1)S(1)} %copy-done.56), kind=kLoop, calls=%fused_computation.2 | loop fusion | flops 37748736 | bytes 63013888 | tf_op jit(solution)/shard_map/convert_element_type | solution.py:220
  537.0 9.9 %fusion.71 = bf16[2,512,12,64]{1,3,2,0:T(8,128)(2,1)} fusion(bf16[2,12,512,512]{2,3,1,0:T(8,128)(2,1)} %multiply_convert_fusion.1, bf16[2,512,12,64]{1,0,3,2:T(2,128)(2,1)S(1)} %copy-done.10), kind=kOutput, calls=%fused_computation.157 | convolution fusion | flops 806879232 | bytes 15728640 | tf_op jit(solution)/shard_map/ihlm,ilhe->imhe/dot_general | solution.py:226
  546.9 6.7 fusion.70
  553.6 22.5 %fusion.141 = (f32[1024]{0:T(1024)S(1)}, f32[1024]{0:T(1024)S(1)}, f32[1024,768]{1,0:T(8,128)}) fusion(f32[1024]{0:T(1024)S(1)} %copy-done.71, f32[1024,768]{1,0:T(8,128)} %copy-done.38, f32[1024]{0:T(1024)S(1)} %copy-done.65, f32[768]{0:T(1024)S(1)} %get-tuple-element.63, f32[1024,768]{1,0:T(8,128)} %get-tuple-element.28, ...), kind=kOutput, calls=%fused_computation.256 | convolution fusion | flops 9717151744 | bytes 44071936 | tf_op jit(solution)/shard_map/tf,df->td/dot_general | solution.py:202
  576.2 5.8 convolution_convert_fusion.4
  586.1 12.6 %fusion.69 = bf16[2,512,12,64]{1,3,2,0:T(8,128)(2,1)} fusion(bf16[2,512,12,64]{1,0,3,2:T(2,128)(2,1)} %reshape.256, f32[2,12,512,512]{2,3,1,0:T(8,128)} %get-tuple-element.43, f32[2,12,512]{2,1,0:T(8,128)S(1)} %copy-done.46, pred[2,512]{1,0:T(4,128)(4,1)S(1)} %copy-done.54), kind=kOutput, calls=%fused_computation.155 | convolution fusion | flops 831258624 | bytes 28361728 | tf_op jit(solution)/shard_map/ihlm,ilhe->imhe/dot_general | solution.py:216
  598.7 21.5 %multiply_reduce_fusion = (f32[2,12,512]{2,1,0:T(8,128)S(1)}, f32[2,12,512,512]{2,3,1,0:T(8,128)}) fusion(f32[2,12,512,512]{2,3,1,0:T(8,128)} %get-tuple-element.43, f32[2,12,512]{2,1,0:T(8,128)S(1)} %copy-done.46, pred[2,512]{1,0:T(4,128)(4,1)S(1)} %copy-done.54, bf16[2,512,12,64]{1,0,3,2:T(2,128)(2,1)S(1)} %copy-done.30, bf16[2,512,12,64]{1,0,3,2:T(2,128)(2,1)} %reshape.256), kind=kOutput, calls=%fused_computation.1 | convolution fusion | flops 836751360 | bytes 53576704 | tf_op jit(solution)/shard_map/ilhe,imhe->ihlm/dot_general | solution.py:213
  620.2 21.8 %multiply_convert_fusion = bf16[2,12,512,512]{2,3,1,0:T(8,128)(2,1)} fusion(f32[2,12,512,512]{2,3,1,0:T(8,128)} %get-tuple-element.57, f32[2,12,512,512]{2,3,1,0:T(8,128)} %get-tuple-element.43, f32[2,12,512]{2,1,0:T(8,128)S(1)} %get-tuple-element.56, f32[2,12,512]{2,1,0:T(8,128)S(1)} %copy-done.46, pred[2,512]{1,0:T(4,128)(4,1)S(1)} %copy-done.54), kind=kLoop, calls=%fused_computation | loop fusion | flops 37748736 | bytes 63013888 | tf_op jit(solution)/shard_map/convert_element_type | solution.py:220
  642.1 9.8 %fusion.73 = bf16[2,512,12,64]{1,3,2,0:T(8,128)(2,1)} fusion(bf16[2,12,512,512]{2,3,1,0:T(8,128)(2,1)} %multiply_convert_fusion, bf16[2,512,12,64]{1,0,3,2:T(2,128)(2,1)S(1)} %copy-done.8), kind=kOutput, calls=%fused_computation.159 | convolution fusion | flops 806879232 | bytes 15728640 | tf_op jit(solution)/shard_map/ihlm,ilhe->imhe/dot_general | solution.py:226
  651.8 6.8 fusion.72
  661.4 3.8 stack_reshape.27
  677.7 4.6 fusion.105
  682.4 3.0 copy.270
  705.2 4.7 fusion.103
  712.4 38.5 %psum.7 = f32[2,8,768]{2,1,0:T(8,128)S(1)} all-reduce(f32[2,8,768]{2,1,0:T(8,128)S(1)} %fusion.101), channel_id=1, replica_groups=mesh['fsdp'=8,'rep'=4] {'fsdp','rep'}, use_global_device_ids=true, to_apply=%region_22.23 | all-reduce | flops 12288 | bytes 98304 | tf_op jit(solution)/shard_map/psum | solution.py:50
  755.5 8.4 %fusion.37 = bf16[1024,768]{1,0:T(8,128)(2,1)S(1)} fusion(f32[1024,768,1]{1,0,2:T(8,128)} %fusion.103, bf16[3,768,768]{2,1,0:T(8,128)(2,1)} %all-gather.9.cloned.1.call-done, bf16[1024,1,768]{2,0,1:T(8,128)(2,1)S(1)} %copy-done.27, bf16[1024,1,768]{2,0,1:T(8,128)(2,1)} %copy.272, bf16[1024,1,768]{2,0,1:T(8,128)(2,1)S(1)} %copy-done.28, ...), kind=kOutput, calls=%fused_computation.83 | convolution fusion | flops 3635675136 | bytes 19283968 | tf_op jit(solution)/shard_map/tke,kde->td/dot_general | solution.py:233
  764.1 6.3 fusion.36
  (284 shorter events, 105.0 us)
Async XLA Ops:
  7.2 140.3 %copy-start = (bf16[2,8,768]{2,1,0:T(8,128)(2,1)S(1)}, bf16[2,8,768]{2,1,0:T(8,128)(2,1)}, u32[]{:S(2)}) copy-start(bf16[2,8,768]{2,1,0:T(8,128)(2,1)} %param.20) | copy-start | bytes 73732
  7.2 173.5 %all-gather.9.cloned.1.call-start = ((), (), s32[]{:S(2)}) async-start(), calls=%async_computation | async-start | bytes 3981312 | tf_op jit(solution)/shard_map/all_gather | solution.py:36
  8.3 73.5 %copy-start.67 = (s32[4,2]{0,1:T(2,128)S(1)}, s32[4,2]{0,1:T(2,128)}, u32[]{:S(2)}) copy-start(s32[4,2]{0,1:T(2,128)} %param.15) | copy-start | bytes 100
  8.3 73.6 %copy-start.78 = (bf16[384]{0:T(512)(128)(2,1)S(1)}, bf16[384]{0:T(512)(128)(2,1)}, u32[]{:S(2)}) copy-start(bf16[384]{0:T(512)(128)(2,1)} %param.24) | copy-start | bytes 2308
  8.3 73.6 %copy-start.87 = (u32[32]{0:T(128)S(1)}, u32[32]{0:T(128)}, u32[]{:S(2)}) copy-start(u32[32]{0:T(128)} %constant.101) | copy-start | bytes 388
  8.3 74.9 %copy-start.86 = (bf16[96]{0:T(256)(128)(2,1)S(1)}, bf16[96]{0:T(256)(128)(2,1)}, u32[]{:S(2)}) copy-start(bf16[96]{0:T(256)(128)(2,1)} %param.26) | copy-start | bytes 580
  8.4 87.8 %copy-start.79 = (bf16[2,96]{1,0:T(2,128)(2,1)S(1)}, bf16[2,96]{1,0:T(2,128)(2,1)}, u32[]{:S(2)}) copy-start(bf16[2,96]{1,0:T(2,128)(2,1)} %param.21) | copy-start | bytes 1156
  8.4 96.5 %copy-start.80 = (bf16[2,96]{1,0:T(2,128)(2,1)S(1)}, bf16[2,96]{1,0:T(2,128)(2,1)}, u32[]{:S(2)}) copy-start(bf16[2,96]{1,0:T(2,128)(2,1)} %param.22) | copy-start | bytes 1156
  8.4 104.6 %copy-start.77 = (bf16[3,96]{1,0:T(4,128)(2,1)S(1)}, bf16[3,96]{1,0:T(4,128)(2,1)}, u32[]{:S(2)}) copy-start(bf16[3,96]{1,0:T(4,128)(2,1)} %param.18) | copy-start | bytes 1732
  8.4 114.5 %copy-start.1 = (bf16[4,512,768]{2,1,0:T(8,128)(2,1)S(1)}, bf16[4,512,768]{2,1,0:T(8,128)(2,1)}, u32[]{:S(2)}) copy-start(bf16[4,512,768]{2,1,0:T(8,128)(2,1)} %param.27) | copy-start | bytes 9437188
  32.4 263.2 %all-gather.11.cloned.1.call-start = ((), (), s32[]{:S(2)}) async-start(), calls=%async_computation.1 | async-start | bytes 1327104 | tf_op jit(solution)/shard_map/all_gather | solution.py:37
  47.8 85.2 %copy-start.76 = (bf16[2,96,8]{1,2,0:T(8,128)(2,1)S(1)}, bf16[2,96,8]{1,2,0:T(8,128)(2,1)}, u32[]{:S(2)}) copy-start(bf16[2,96,8]{1,2,0:T(8,128)(2,1)} %param.19) | copy-start | bytes 9220
  47.8 293.8 %all-gather.13.cloned.1.call-start = ((), (), s32[]{:S(2)}) async-start(), calls=%async_computation.2 | async-start | bytes 5308416 | tf_op jit(solution)/shard_map/all_gather | solution.py:38
  65.3 348.4 %all-gather.15.cloned.1.call-start = ((), (), s32[]{:S(2)}) async-start(), calls=%async_computation.3 | async-start | bytes 5308416 | tf_op jit(solution)/shard_map/all_gather | solution.py:39
  122.9 10.1 %copy-start.57 = (f32[768]{0:T(1024)}, f32[768]{0:T(1024)S(1)}, u32[]{:S(2)}) copy-start(f32[768]{0:T(1024)S(1)} %get-tuple-element.64) | copy-start | bytes 9220
  145.7 18.3 %copy-start.51 = (bf16[1024,2,8]{0,2,1:T(8,128)(2,1)}, bf16[1024,2,8]{0,2,1:T(8,128)(2,1)S(1)}, u32[]{:S(2)}) copy-start(bf16[1024,2,8]{0,2,1:T(8,128)(2,1)S(1)} %fusion.99) | copy-start | bytes 98308
  180.7 99.8 %copy-start.55 = (pred[2,512]{1,0:T(4,128)(4,1)}, pred[2,512]{1,0:T(4,128)(4,1)S(1)}, u32[]{:S(2)}) copy-start(pred[2,512]{1,0:T(4,128)(4,1)S(1)} %get-tuple-element.62) | copy-start | bytes 3076
  180.7 143.3 %copy-start.53 = (pred[2,512]{1,0:T(4,128)(4,1)}, pred[2,512]{1,0:T(4,128)(4,1)S(1)}, u32[]{:S(2)}) copy-start(pred[2,512]{1,0:T(4,128)(4,1)S(1)} %get-tuple-element.61) | copy-start | bytes 3076
  188.3 4.7 copy-start.82
  210.4 89.1 %copy-start.3 = (bf16[2,512,12,64]{1,0,3,2:T(2,128)(2,1)}, bf16[2,512,12,64]{1,0,3,2:T(2,128)(2,1)S(1)}, u32[]{:S(2)}) copy-start(bf16[2,512,12,64]{1,0,3,2:T(2,128)(2,1)S(1)} %convert_element_type.220) | copy-start | bytes 4718596
  223.8 5.8 copy-start.17
  234.5 17.6 %copy-start.5 = (bf16[2,512,12,64]{1,0,3,2:T(2,128)(2,1)}, bf16[2,512,12,64]{1,0,3,2:T(2,128)(2,1)S(1)}, u32[]{:S(2)}) copy-start(bf16[2,512,12,64]{1,0,3,2:T(2,128)(2,1)S(1)} %convert_element_type.205) | copy-start | bytes 4718596
  252.1 11.1 %copy-start.9 = (bf16[2,512,12,64]{1,0,3,2:T(2,128)(2,1)}, bf16[2,512,12,64]{1,0,3,2:T(2,128)(2,1)S(1)}, u32[]{:S(2)}) copy-start(bf16[2,512,12,64]{1,0,3,2:T(2,128)(2,1)S(1)} %get-tuple-element.36) | copy-start | bytes 4718596
  263.2 12.9 %copy-start.11 = (f32[2,512,12,64]{1,0,3,2:T(2,128)S(1)}, f32[2,512,12,64]{1,0,3,2:T(2,128)}, u32[]{:S(2)}) copy-start(f32[2,512,12,64]{1,0,3,2:T(2,128)} %mul.311) | copy-start | bytes 9437188
  263.2 12.9 %copy-start.12 = (f32[2,512,12,64]{1,0,3,2:T(2,128)S(1)}, f32[2,512,12,64]{1,0,3,2:T(2,128)}, u32[]{:S(2)}) copy-start(f32[2,512,12,64]{1,0,3,2:T(2,128)} %mul.331) | copy-start | bytes 9437188
  263.2 12.9 %copy-start.13 = (f32[2,512,12,64]{1,0,3,2:T(2,128)S(1)}, f32[2,512,12,64]{1,0,3,2:T(2,128)}, u32[]{:S(2)}) copy-start(f32[2,512,12,64]{1,0,3,2:T(2,128)} %squeeze.10) | copy-start | bytes 9437188
  263.2 12.9 %copy-start.14 = (f32[2,512,12,64]{1,0,3,2:T(2,128)S(1)}, f32[2,512,12,64]{1,0,3,2:T(2,128)}, u32[]{:S(2)}) copy-start(f32[2,512,12,64]{1,0,3,2:T(2,128)} %squeeze.8) | copy-start | bytes 9437188
  276.1 4.4 copy-start.47
  280.5 11.9 %copy-start.31 = (bf16[2,512,12,64]{1,0,3,2:T(2,128)(2,1)}, bf16[2,512,12,64]{1,0,3,2:T(2,128)(2,1)S(1)}, u32[]{:S(2)}) copy-start(bf16[2,512,12,64]{1,0,3,2:T(2,128)(2,1)S(1)} %get-tuple-element.38) | copy-start | bytes 4718596
  299.0 13.7 %copy-start.34 = (f32[1024,768]{1,0:T(8,128)}, f32[1024,768]{1,0:T(8,128)S(1)}, u32[]{:S(2)}) copy-start(f32[1024,768]{1,0:T(8,128)S(1)} %get-tuple-element.47) | copy-start | bytes 9437188
  299.0 175.0 %copy-start.60 = (f32[1024]{0:T(1024)}, f32[1024]{0:T(1024)S(1)}, u32[]{:S(2)}) copy-start(f32[1024]{0:T(1024)S(1)} %broadcast_multiply_fusion.10) | copy-start | bytes 12292
  299.6 174.5 %copy-start.68 = (f32[1024]{0:T(1024)}, f32[1024]{0:T(1024)S(1)}, u32[]{:S(2)}) copy-start(f32[1024]{0:T(1024)S(1)} %add_rsqrt_fusion.3) | copy-start | bytes 12292
  312.7 11.3 %copy-start.29 = (bf16[2,512,12,64]{1,0,3,2:T(2,128)(2,1)S(1)}, bf16[2,512,12,64]{1,0,3,2:T(2,128)(2,1)}, u32[]{:S(2)}) copy-start(bf16[2,512,12,64]{1,0,3,2:T(2,128)(2,1)} %get-tuple-element.39) | copy-start | bytes 4718596
  324.0 11.6 %copy-start.45 = (f32[2,12,512]{2,1,0:T(8,128)}, f32[2,12,512]{2,1,0:T(8,128)S(1)}, u32[]{:S(2)}) copy-start(f32[2,12,512]{2,1,0:T(8,128)S(1)} %log_add_fusion) | copy-start | bytes 147460
  339.4 10.5 %copy-start.64 = (f32[1024]{0:T(1024)}, f32[1024]{0:T(1024)S(1)}, u32[]{:S(2)}) copy-start(f32[1024]{0:T(1024)S(1)} %broadcast_multiply_fusion.8) | copy-start | bytes 12292
  341.5 8.4 %copy-start.70 = (f32[1024]{0:T(1024)}, f32[1024]{0:T(1024)S(1)}, u32[]{:S(2)}) copy-start(f32[1024]{0:T(1024)S(1)} %add_rsqrt_fusion.1) | copy-start | bytes 12292
  341.6 12.9 %copy-start.35 = (f32[1024,768]{1,0:T(8,128)S(1)}, f32[1024,768]{1,0:T(8,128)}, u32[]{:S(2)}) copy-start(f32[1024,768]{1,0:T(8,128)} %copy-done.34) | copy-start | bytes 9437188
  341.6 12.9 %copy-start.81 = (bf16[768,3072]{1,0:T(8,128)(2,1)S(1)}, bf16[768,3072]{1,0:T(8,128)(2,1)}, u32[]{:S(2)}) copy-start(bf16[768,3072]{1,0:T(8,128)(2,1)} %all-gather.13.cloned.1.call-done) | copy-start | bytes 14155780
  349.9 4.5 copy-start.88
  354.5 59.2 %copy-start.66 = (f32[768]{0:T(1024)S(1)}, f32[768]{0:T(1024)}, u32[]{:S(2)}) copy-start(f32[768]{0:T(1024)} %convert_element_type.214) | copy-start | bytes 9220
  451.9 22.8 %copy-start.36 = (f32[1024,768]{1,0:T(8,128)S(1)}, f32[1024,768]{1,0:T(8,128)}, u32[]{:S(2)}) copy-start(f32[1024,768]{1,0:T(8,128)} %copy-done.34) | copy-start | bytes 9437188
  482.9 12.8 %copy-start.32 = (bf16[2,512,12,64]{1,0,3,2:T(2,128)(2,1)S(1)}, bf16[2,512,12,64]{1,0,3,2:T(2,128)(2,1)}, u32[]{:S(2)}) copy-start(bf16[2,512,12,64]{1,0,3,2:T(2,128)(2,1)} %copy-done.31) | copy-start | bytes 4718596
  515.4 21.6 %copy-start.10 = (bf16[2,512,12,64]{1,0,3,2:T(2,128)(2,1)S(1)}, bf16[2,512,12,64]{1,0,3,2:T(2,128)(2,1)}, u32[]{:S(2)}) copy-start(bf16[2,512,12,64]{1,0,3,2:T(2,128)(2,1)} %copy-done.9) | copy-start | bytes 4718596
  537.0 9.9 %copy-start.6 = (bf16[2,512,12,64]{1,0,3,2:T(2,128)(2,1)S(1)}, bf16[2,512,12,64]{1,0,3,2:T(2,128)(2,1)}, u32[]{:S(2)}) copy-start(bf16[2,512,12,64]{1,0,3,2:T(2,128)(2,1)} %copy-done.5) | copy-start | bytes 4718596
  553.6 22.5 %copy-start.85 = (bf16[768,768]{1,0:T(8,128)(2,1)S(1)}, bf16[768,768]{1,0:T(8,128)(2,1)}, u32[]{:S(2)}) copy-start(bf16[768,768]{1,0:T(8,128)(2,1)} %all-gather.11.cloned.1.call-done) | copy-start | bytes 3538948
  586.1 12.6 %copy-start.30 = (bf16[2,512,12,64]{1,0,3,2:T(2,128)(2,1)S(1)}, bf16[2,512,12,64]{1,0,3,2:T(2,128)(2,1)}, u32[]{:S(2)}) copy-start(bf16[2,512,12,64]{1,0,3,2:T(2,128)(2,1)} %get-tuple-element.39) | copy-start | bytes 4718596
  620.2 21.8 %copy-start.8 = (bf16[2,512,12,64]{1,0,3,2:T(2,128)(2,1)S(1)}, bf16[2,512,12,64]{1,0,3,2:T(2,128)(2,1)}, u32[]{:S(2)}) copy-start(bf16[2,512,12,64]{1,0,3,2:T(2,128)(2,1)} %get-tuple-element.37) | copy-start | bytes 4718596
  642.1 9.8 %copy-start.4 = (bf16[2,512,12,64]{1,0,3,2:T(2,128)(2,1)S(1)}, bf16[2,512,12,64]{1,0,3,2:T(2,128)(2,1)}, u32[]{:S(2)}) copy-start(bf16[2,512,12,64]{1,0,3,2:T(2,128)(2,1)} %copy-done.3) | copy-start | bytes 4718596
  651.8 6.8 copy-start.42
  670.5 4.6 copy-start.52
  673.4 4.3 copy-start.44
  705.1 4.7 copy-start.50
  705.1 48.4 %copy-start.61 = (f32[1024]{0:T(1024)S(1)}, f32[1024]{0:T(1024)}, u32[]{:S(2)}) copy-start(f32[1024]{0:T(1024)} %copy-done.60) | copy-start | bytes 12292
  705.1 48.3 %copy-start.69 = (f32[1024]{0:T(1024)S(1)}, f32[1024]{0:T(1024)}, u32[]{:S(2)}) copy-start(f32[1024]{0:T(1024)} %copy-done.68) | copy-start | bytes 12292
  705.2 48.3 %copy-start.73 = (f32[1024]{0:T(1024)S(1)}, f32[1024]{0:T(1024)}, u32[]{:S(2)}) copy-start(f32[1024]{0:T(1024)} %copy-done.72) | copy-start | bytes 12292
  705.2 48.3 %copy-start.75 = (f32[1024]{0:T(1024)S(1)}, f32[1024]{0:T(1024)}, u32[]{:S(2)}) copy-start(f32[1024]{0:T(1024)} %copy-done.74) | copy-start | bytes 12292
  709.9 41.7 %copy-start.15 = (bf16[1024,768]{1,0:T(8,128)(2,1)S(1)}, bf16[1024,768]{1,0:T(8,128)(2,1)}, u32[]{:S(2)}) copy-start(bf16[1024,768]{1,0:T(8,128)(2,1)} %get-tuple-element.29) | copy-start | bytes 4718596
  709.9 41.7 %copy-start.16 = (bf16[1024,768]{1,0:T(8,128)(2,1)S(1)}, bf16[1024,768]{1,0:T(8,128)(2,1)}, u32[]{:S(2)}) copy-start(bf16[1024,768]{1,0:T(8,128)(2,1)} %get-tuple-element.30) | copy-start | bytes 4718596
  755.5 8.4 %copy-start.24 = (bf16[1024,1,768]{2,0,1:T(8,128)(2,1)S(1)}, bf16[1024,1,768]{2,0,1:T(8,128)(2,1)}, u32[]{:S(2)}) copy-start(bf16[1024,1,768]{2,0,1:T(8,128)(2,1)} %copy.291) | copy-start | bytes 4718596
  755.5 8.4 %copy-start.25 = (bf16[1024,1,768]{2,0,1:T(8,128)(2,1)S(1)}, bf16[1024,1,768]{2,0,1:T(8,128)(2,1)}, u32[]{:S(2)}) copy-start(bf16[1024,1,768]{2,0,1:T(8,128)(2,1)} %copy.289) | copy-start | bytes 4718596
  755.5 8.4 %copy-start.39 = (f32[1024,768]{1,0:T(8,128)S(1)}, f32[1024,768]{1,0:T(8,128)}, u32[]{:S(2)}) copy-start(f32[1024,768]{1,0:T(8,128)} %copy-done.38) | copy-start | bytes 9437188
  755.5 8.4 %copy-start.40 = (f32[1024,768,1]{1,0,2:T(8,128)S(1)}, f32[1024,768,1]{1,0,2:T(8,128)}, u32[]{:S(2)}) copy-start(f32[1024,768,1]{1,0,2:T(8,128)} %fusion.105) | copy-start | bytes 9437188
  755.5 8.4 %copy-start.41 = (bf16[1024,1,768]{2,0,1:T(8,128)(2,1)S(1)}, bf16[1024,1,768]{2,0,1:T(8,128)(2,1)}, u32[]{:S(2)}) copy-start(bf16[1024,1,768]{2,0,1:T(8,128)(2,1)} %copy.290) | copy-start | bytes 4718596
  755.5 8.5 %copy-start.83 = (bf16[3,768,768]{2,1,0:T(8,128)(2,1)S(1)}, bf16[3,768,768]{2,1,0:T(8,128)(2,1)}, u32[]{:S(2)}) copy-start(bf16[3,768,768]{2,1,0:T(8,128)(2,1)} %all-gather.9.cloned.1.call-done) | copy-start | bytes 10616836
  (29 other events, 63.2 us)
Sparse Core Ops, SparseCore 0:
  32.5 33.4 all-gather.8
  67.9 24.0 all-gather.10
  93.9 38.7 all-gather.12
  134.4 39.6 all-gather.14
where the time goes:
time: 784 us; the launch traced here: 779 us
  matrix products  345 us (44%)
  blocking collectives  163 us (21%)
  local copies, waits for them, and re-layouts  154 us (20%)
  other arithmetic  101 us (13%)
  between operations  15.9 us (2%)
    dot_general x2, matrix products, forward_sweep(): jnp.dot(hidden_one.astype(jnp.bfloat16), in_full, preferred_element_type=...  67.6 us
    dot_general x2, matrix products, reverse_sweep(): jnp.einsum('tf,df->td', grad_inner, in_full, preferred_element_type=jnp.f...  44.6 us
    convert_element_type x2, other arithmetic, reverse_sweep(): grad_scores = (attn_weights * (grad_probs - row_inner)).astype(jnp.bfloat16)  43.4 us
    dot_general x2, matrix products, reverse_sweep(): jnp.einsum('ilhe,imhe->ihlm', grad_mixed, value_bf, preferred_element_typ...  41.2 us
    psum x1, blocking collectives, adapter_sum(): return lax.psum(adapter_grad_term, ('fsdp', 'rep'))  38.5 us
    dot_general x2, matrix products, forward_sweep(): jnp.dot(activation, back_full, preferred_element_type=jnp.float32)  28.6 us
    dot_general x2, matrix products, reverse_sweep(): jnp.einsum('ihlm,ilhe->imhe', probs_bf, grad_mixed, preferred_element_typ...  25.4 us
    another operation x12, local copies, waits for them, and re-layouts, reverse_sweep(): grad_proj = jnp.stack([query_gradient, grad_key, value_gradient], axis=1)  24.3 us
  transfers between devices with their start and end apart: 4, of which 0 were waited for; matrix products, arithmetic and copies ran while one was open for 34% of the time, Pallas kernels for 0%

commit v1 on v0

--- a/solution.py
+++ b/solution.py
@@ -11,6 +11,27 @@
 ADAPTER_ALPHA = 16
 L = 512
 MB = 2
+
+
+def ring_gather(x, axis, dim):
+    peers, index, rows = (lax.axis_size(axis), lax.axis_index(axis), x.shape[dim])
+    right = [(i, (i + 1) % peers) for i in range(peers)]
+    downward = [(i, (i - 1) % peers) for i in range(peers)]
+    whole = jnp.zeros((*x.shape[:dim], peers * rows, *x.shape[dim + 1 :]), x.dtype)
+    whole = lax.dynamic_update_slice_in_dim(whole, x, index * rows, axis=dim)
+    from_left = from_right = x
+    half = peers // 2
+    for lap in range(1, half + 1):
+        from_left = lax.ppermute(from_left, axis, right)
+        whole = lax.dynamic_update_slice_in_dim(
+            whole, from_left, (index - lap) % peers * rows, axis=dim
+        )
+        if lap < peers - half:
+            from_right = lax.ppermute(from_right, axis, downward)
+            whole = lax.dynamic_update_slice_in_dim(
+                whole, from_right, (index + lap) % peers * rows, axis=dim
+            )
+    return whole
 
 
 def collect_frozen(frozen_args):
@@ -27,7 +48,7 @@
         back_bias_part,
     ) = frozen_args
     columns = (
-        lax.all_gather(qkv_part, "rep", axis=2, tiled=True),
+        ring_gather(qkv_part, "rep", 2),
         lax.all_gather(out_part, "rep", axis=1, tiled=True),
         lax.all_gather(in_part, "rep", axis=1, tiled=True),
         lax.all_gather(back_part, "rep", axis=1, tiled=True),

time: 784 us -> 765 us (0.976)
  blocking collectives: 163 us -> 144 us
  local copies, waits for them, and re-layouts: 154 us -> 144 us
    all_gather x1 -> x0, blocking collectives: 21.9 us -> none  [collect_frozen(): lax.all_gather(qkv_part, 'rep', axis=2, tiled=True)]
    slice x2 -> x0, local copies, waits for them, and re-layouts: 8.27 us -> none  [forward_sweep(): projected_rows[:, 2] + attention_single[1]]
    dynamic_update_slice x0 -> x4, local copies, waits for them, and re-layouts: none -> 8.15 us  [the longest x2 3.76 us: ring_gather(): lax.dynamic_update_slice_in_dim(whole, from_left, (index - lap) % peers *...]
    unnamed x189 -> x186, local copies, waits for them, and re-layouts: 21.2 us -> 19.9 us
  transfers between devices with their start and end apart: 4 -> 7, of which waited for: 0 -> 1; matrix products, arithmetic and copies ran while one was open for 34% -> 34% of each run, Pallas kernels for 0% -> 0%
where the time goes in v1:
time: 765 us; the launch traced here: 760 us
  matrix products  345 us (45%)
  local copies, waits for them, and re-layouts  144 us (19%)
  blocking collectives  144 us (19%)
  other arithmetic  101 us (13%)
  between operations  15.9 us (2%)
    dot_general x2, matrix products, forward_sweep(): jnp.dot(hidden_one.astype(jnp.bfloat16), in_full, preferred_element_type=...  67.5 us
    dot_general x2, matrix products, reverse_sweep(): jnp.einsum('tf,df->td', grad_inner, in_full, preferred_element_type=jnp.f...  44.5 us
    convert_element_type x2, other arithmetic, reverse_sweep(): grad_scores = (attn_weights * (grad_probs - row_inner)).astype(jnp.bfloat16)  43.6 us
    dot_general x2, matrix products, reverse_sweep(): jnp.einsum('ilhe,imhe->ihlm', grad_mixed, value_bf, preferred_element_typ...  41.3 us
    psum x1, blocking collectives, adapter_sum(): return lax.psum(adapter_grad_term, ('fsdp', 'rep'))  38.5 us
    dot_general x2, matrix products, forward_sweep(): jnp.dot(activation, back_full, preferred_element_type=jnp.float32)  28.8 us
    dot_general x2, matrix products, reverse_sweep(): jnp.einsum('ihlm,ilhe->imhe', probs_bf, grad_mixed, preferred_element_typ...  25.3 us
    another operation x12, local copies, waits for them, and re-layouts, reverse_sweep(): grad_proj = jnp.stack([query_gradient, grad_key, value_gradient], axis=1)  24.3 us
  transfers between devices with their start and end apart: 7, of which 1 were waited for; matrix products, arithmetic and copies ran while one was open for 34% of the time, Pallas kernels for 0%

profile of v1, /device:TPU:0, one launch (start us, length us, event | category | flops | bytes accessed | tf_op | source)
XLA Modules:
  0.0 759.8 jit_solution(9382113463821285745)
XLA Ops:
  7.3 3.1 collective-permute-start
  12.5 4.9 collective-permute-done
  27.3 15.9 %all_gather.29 = bf16[96,768]{0,1:T(8,128)(2,1)S(1)} all-gather(bf16[96,192]{0,1:T(8,128)(2,1)S(1)} %copy.217), channel_id=1, replica_groups=mesh['fsdp'=8,'rep'=4] {'rep'}, dimensions={1}, use_global_device_ids=true | all-gather | bytes 184320 | tf_op jit(solution)/shard_map/all_gather | solution.py:52
  44.1 17.1 %all_gather.33 = bf16[96,3072]{1,0:T(8,128)(2,1)} all-gather(bf16[96,768]{1,0:T(8,128)(2,1)} %param.23), channel_id=1, replica_groups=mesh['fsdp'=8,'rep'=4] {'rep'}, dimensions={1}, use_global_device_ids=true | all-gather | bytes 737280 | tf_op jit(solution)/shard_map/all_gather | solution.py:53
  61.3 16.2 %all_gather.36 = bf16[384,768]{0,1:T(8,128)(2,1)} all-gather(bf16[384,192]{0,1:T(8,128)(2,1)} %param.25), channel_id=1, replica_groups=mesh['fsdp'=8,'rep'=4] {'rep'}, dimensions={1}, use_global_device_ids=true | all-gather | bytes 737280 | tf_op jit(solution)/shard_map/all_gather | solution.py:54
  79.2 12.0 %all-reduce = bf16[768]{0:T(1024)(128)(2,1)S(1)} all-reduce(bf16[768]{0:T(1024)(128)(2,1)S(1)} %dynamic-update-slice), channel_id=1, replica_groups=mesh['fsdp'=8,'rep'=4] {'fsdp'}, use_global_device_ids=true, to_apply=%add | all-reduce | flops 768 | bytes 3072
  91.8 8.9 %all-gather.1 = bf16[8,96,2]{1,2,0:T(2,128)(2,1)S(1)} all-gather(bf16[1,96,2]{1,2,0:T(2,128)(2,1)S(1)} %bitcast.233), channel_id=1, replica_groups=mesh['fsdp'=8,'rep'=4] {'fsdp'}, dimensions={0}, use_global_device_ids=true | all-gather | bytes 3456 | tf_op jit(solution)/shard_map/all_gather | solution.py:63
  100.7 7.8 %all-gather.2 = bf16[8,96,2]{1,2,0:T(2,128)(2,1)S(1)} all-gather(bf16[1,96,2]{1,2,0:T(2,128)(2,1)S(1)} %bitcast.234), channel_id=1, replica_groups=mesh['fsdp'=8,'rep'=4] {'fsdp'}, dimensions={0}, use_global_device_ids=true | all-gather | bytes 3456 | tf_op jit(solution)/shard_map/all_gather | solution.py:64
  108.6 9.2 %all-gather = bf16[8,96,3]{1,2,0:T(4,128)(2,1)S(1)} all-gather(bf16[1,96,3]{1,2,0:T(4,128)(2,1)S(1)} %bitcast.232), channel_id=1, replica_groups=mesh['fsdp'=8,'rep'=4] {'fsdp'}, dimensions={0}, use_global_device_ids=true | all-gather | bytes 5184 | tf_op jit(solution)/shard_map/all_gather | solution.py:61
  120.6 7.9 %all-gather.3 = bf16[8,1,384]{2,1,0:T(2,128)(2,1)S(1)} all-gather(bf16[1,1,384]{2,1,0:T(2,128)(2,1)S(1)} %reshape.269), channel_id=1, replica_groups=mesh['fsdp'=8,'rep'=4] {'fsdp'}, dimensions={0}, use_global_device_ids=true | all-gather | bytes 6912 | tf_op jit(solution)/shard_map/all_gather | solution.py:65
  128.7 10.2 %all_gather.28 = bf16[2,768,8]{2,0,1:T(2,128)(2,1)S(1)} all-gather(bf16[2,96,8]{2,0,1:T(2,128)(2,1)S(1)} %copy.208), channel_id=1, replica_groups=mesh['fsdp'=8,'rep'=4] {'fsdp'}, dimensions={1}, use_global_device_ids=true | all-gather | bytes 27648 | tf_op jit(solution)/shard_map/all_gather | solution.py:62
  144.7 3.1 slice_multiply_fusion.2
  150.2 3.8 mul.341
  156.5 3.7 mul.339
  161.2 3.1 slice_multiply_fusion
  166.7 3.8 mul.361
  172.8 3.9 mul.359
  176.9 6.4 convolution_bitcast_fusion
  183.5 3.8 fusion.143
  188.2 3.9 convolution_bitcast_fusion.1
  193.5 3.3 fusion.142
  198.0 6.2 squeeze.11
  204.1 5.6 squeeze.10
  209.8 3.1 convert_element_type.205
  212.8 6.2 squeeze.9
  219.1 5.6 squeeze.8
  224.6 7.9 %add_convert_fusion.8 = (bf16[2,512,12,64]{1,0,3,2:T(2,128)(2,1)S(1)}, bf16[2,512,12,64]{1,0,3,2:T(2,128)(2,1)}) fusion(f32[2,512,12,64]{1,0,3,2:T(2,128)} %mul.341, f32[2,512,12,64]{1,0,3,2:T(2,128)} %squeeze.9, f32[12,64]{1,0:T(8,128)S(1)} %add.284, f32[2,512,12,64]{1,0,3,2:T(2,128)} %mul.361, f32[2,512,12,64]{1,0,3,2:T(2,128)} %squeeze.11), kind=kLoop, calls=%fused_computation.118 | loop fusion | flops 4718592 | bytes 15731712 | tf_op jit(solution)/shard_map/convert_element_type | solution.py:132
  232.6 11.1 %fusion = (f32[2,12,512]{2,1,0:T(8,128)S(1)}, f32[2,12,512,512]{2,3,1,0:T(8,128)}) fusion(pred[2,512]{1,0:T(4,128)(4,1)S(1)} %get-tuple-element.62, bf16[2,512,12,64]{1,0,3,2:T(2,128)(2,1)S(1)} %convert_element_type.205, bf16[2,512,12,64]{1,0,3,2:T(2,128)(2,1)S(1)} %get-tuple-element.36), kind=kOutput, calls=%fused_computation.10 | convolution fusion | flops 824168448 | bytes 28361728 | tf_op jit(solution)/shard_map/ilhe,imhe->ihlm/dot_general | solution.py:97
  243.7 12.8 %exponential_reduce_fusion.1 = f32[2,12,512]{2,1,0:T(8,128)S(1)} fusion(f32[2,12,512,512]{2,3,1,0:T(8,128)} %get-tuple-element.45, f32[2,12,512]{2,1,0:T(8,128)S(1)} %get-tuple-element.44, pred[2,512]{1,0:T(4,128)(4,1)S(1)} %get-tuple-element.62), kind=kLoop, calls=%fused_computation.8 | loop fusion | flops 25153536 | bytes 25265152 | tf_op jit(solution)/shard_map/reduce_sum | solution.py:143
  256.6 4.4 add_convert_fusion.9
  261.0 12.2 %fusion.66 = bf16[2,512,12,64]{1,3,2,0:T(8,128)(2,1)S(1)} fusion(bf16[2,512,12,64]{1,0,3,2:T(2,128)(2,1)S(1)} %get-tuple-element.38, f32[2,12,512,512]{2,3,1,0:T(8,128)} %get-tuple-element.45, f32[2,12,512]{2,1,0:T(8,128)S(1)} %log_add_fusion.1, pred[2,512]{1,0:T(4,128)(4,1)S(1)} %get-tuple-element.62), kind=kOutput, calls=%fused_computation.154 | convolution fusion | flops 831258624 | bytes 28361728 | tf_op jit(solution)/shard_map/ihlm,imhe->ilhe/dot_general | solution.py:146
  276.4 3.4 fusion.145
  282.4 11.1 %fusion.1 = (f32[2,12,512]{2,1,0:T(8,128)S(1)}, f32[2,12,512,512]{2,3,1,0:T(8,128)}) fusion(pred[2,512]{1,0:T(4,128)(4,1)S(1)} %get-tuple-element.61, bf16[2,512,12,64]{1,0,3,2:T(2,128)(2,1)S(1)} %convert_element_type.220, bf16[2,512,12,64]{1,0,3,2:T(2,128)(2,1)S(1)} %copy-done.7), kind=kOutput, calls=%fused_computation.11 | convolution fusion | flops 824168448 | bytes 28361728 | tf_op jit(solution)/shard_map/ilhe,imhe->ihlm/dot_general | solution.py:97
  293.5 11.2 %exponential_reduce_fusion = f32[2,12,512]{2,1,0:T(8,128)S(1)} fusion(f32[2,12,512,512]{2,3,1,0:T(8,128)} %get-tuple-element.43, f32[2,12,512]{2,1,0:T(8,128)S(1)} %get-tuple-element.42, pred[2,512]{1,0:T(4,128)(4,1)S(1)} %get-tuple-element.61), kind=kLoop, calls=%fused_computation.5 | loop fusion | flops 25153536 | bytes 25265152 | tf_op jit(solution)/shard_map/reduce_sum | solution.py:143
  304.8 11.3 %fusion.67 = bf16[2,512,12,64]{1,3,2,0:T(8,128)(2,1)S(1)} fusion(bf16[2,512,12,64]{1,0,3,2:T(2,128)(2,1)S(1)} %copy-done.28, f32[2,12,512,512]{2,3,1,0:T(8,128)} %get-tuple-element.43, f32[2,12,512]{2,1,0:T(8,128)S(1)} %log_add_fusion, pred[2,512]{1,0:T(4,128)(4,1)S(1)} %get-tuple-element.61), kind=kOutput, calls=%fused_computation.155 | convolution fusion | flops 831258624 | bytes 28361728 | tf_op jit(solution)/shard_map/ihlm,imhe->ilhe/dot_general | solution.py:146
  322.1 8.3 %fusion.48 = f32[1024,3072]{1,0:T(8,128)S(1)} fusion(bf16[768,3072]{1,0:T(8,128)(2,1)} %all-gather.13.cloned.1.call-done, f32[1024,768]{1,0:T(8,128)} %copy-done.37, f32[1024]{0:T(1024)S(1)} %add_rsqrt_fusion.1, f32[1024]{0:T(1024)S(1)} %broadcast_multiply_fusion.8, f32[768]{0:T(1024)S(1)} %get-tuple-element.17, f32[768]{0:T(1024)S(1)} %get-tuple-element.63), kind=kOutput, calls=%fused_computation.138 | convolution fusion | flops 4835770368 | bytes 20461568 | tf_op jit(solution)/shard_map/dot_general | solution.py:159
  330.5 4.5 copy-done.87
  335.0 59.2 %fusion.4 = (f32[1024,3072]{1,0:T(8,128)}, f32[1024,3072]{1,0:T(8,128)}, f32[1024,3072]{1,0:T(8,128)}) fusion(f32[3072]{0:T(1024)S(1)} %bitcast.227, f32[1024,3072]{1,0:T(8,128)S(1)} %fusion.48, bf16[768,3072]{1,0:T(8,128)(2,1)S(1)} %copy-done.80, f32[1024,768]{1,0:T(8,128)S(1)} %copy-done.34, f32[768]{0:T(1024)S(1)} %get-tuple-element.17, ...), kind=kOutput, calls=%fused_computation.16 | convolution fusion | flops 5232132096 | bytes 58222592 | tf_op jit(solution)/shard_map/dot_general | solution.py:159
  394.2 12.5 %fusion.147 = (f32[1024]{0:T(1024)S(1)}, f32[1024,768]{1,0:T(8,128)S(1)}) fusion(f32[768]{0:T(1024)S(1)} %copy-done.65, bf16[3072,768]{0,1:T(8,128)(2,1)} %all-gather.15.cloned.1.call-done, f32[1024,3072]{1,0:T(8,128)} %get-tuple-element.34, f32[1024,3072]{1,0:T(8,128)} %get-tuple-element.50, f32[3072]{0:T(1024)S(1)} %bitcast.228, ...), kind=kOutput, calls=%fused_computation.264 | convolution fusion | flops 4849925120 | bytes 36209664 | tf_op jit(solution)/shard_map/dot_general | solution.py:165
  407.5 16.3 %fusion.148 = (f32[1024]{0:T(1024)S(1)}, f32[1024,768]{1,0:T(8,128)S(1)}) fusion(f32[768]{0:T(1024)S(1)} %copy-done.65, bf16[3072,768]{0,1:T(8,128)(2,1)} %all-gather.15.cloned.1.call-done, f32[1024,3072]{1,0:T(8,128)} %get-tuple-element.35, f32[1024,3072]{1,0:T(8,128)} %copy-done.87, f32[3072]{0:T(1024)S(1)} %bitcast.229, f32[768]{0:T(1024)S(1)} %get-tuple-element.17, ...), kind=kOutput, calls=%fused_computation.265 | convolution fusion | flops 4849925120 | bytes 36209664 | tf_op jit(solution)/shard_map/dot_general | solution.py:165
  427.8 4.8 subtract_multiply_fusion.1
  432.6 22.2 %fusion.140 = (f32[1024]{0:T(1024)S(1)}, f32[1024]{0:T(1024)S(1)}, f32[1024,768]{1,0:T(8,128)}) fusion(f32[1024]{0:T(1024)S(1)} %add_rsqrt_fusion.3, f32[1024,768]{1,0:T(8,128)} %copy-done.33, f32[1024]{0:T(1024)S(1)} %broadcast_multiply_fusion.10, f32[768]{0:T(1024)S(1)} %get-tuple-element.63, f32[1024,768]{1,0:T(8,128)} %get-tuple-element.31, ...), kind=kOutput, calls=%fused_computation.257 | convolution fusion | flops 9717151744 | bytes 44071936 | tf_op jit(solution)/shard_map/tf,df->td/dot_general | solution.py:223
  455.4 5.3 convolution_convert_fusion.5
  463.7 12.7 %fusion.68 = bf16[2,512,12,64]{1,3,2,0:T(8,128)(2,1)} fusion(bf16[2,512,12,64]{1,0,3,2:T(2,128)(2,1)S(1)} %reshape.254, f32[2,12,512,512]{2,3,1,0:T(8,128)} %get-tuple-element.45, f32[2,12,512]{2,1,0:T(8,128)S(1)} %copy-done.47, pred[2,512]{1,0:T(4,128)(4,1)S(1)} %copy-done.55), kind=kOutput, calls=%fused_computation.156 | convolution fusion | flops 831258624 | bytes 28361728 | tf_op jit(solution)/shard_map/ihlm,ilhe->imhe/dot_general | solution.py:237
  476.4 19.7 %multiply_reduce_fusion.1 = (f32[2,12,512]{2,1,0:T(8,128)S(1)}, f32[2,12,512,512]{2,3,1,0:T(8,128)}) fusion(f32[2,12,512,512]{2,3,1,0:T(8,128)} %get-tuple-element.45, f32[2,12,512]{2,1,0:T(8,128)S(1)} %copy-done.47, pred[2,512]{1,0:T(4,128)(4,1)S(1)} %copy-done.55, bf16[2,512,12,64]{1,0,3,2:T(2,128)(2,1)S(1)} %copy-done.31, ...), kind=kOutput, calls=%fused_computation.3 | convolution fusion | flops 836751360 | bytes 53576704 | tf_op jit(solution)/shard_map/ilhe,imhe->ihlm/dot_general | solution.py:234
  496.2 21.6 %multiply_convert_fusion.1 = bf16[2,12,512,512]{2,3,1,0:T(8,128)(2,1)} fusion(f32[2,12,512,512]{2,3,1,0:T(8,128)} %get-tuple-element.60, f32[2,12,512,512]{2,3,1,0:T(8,128)} %get-tuple-element.45, f32[2,12,512]{2,1,0:T(8,128)S(1)} %get-tuple-element.59, f32[2,12,512]{2,1,0:T(8,128)S(1)} %copy-done.47, pred[2,512]{1,0:T(4,128)(4,1)S(1)} %copy-done.55), kind=kLoop, calls=%fused_computation.2 | loop fusion | flops 37748736 | bytes 63013888 | tf_op jit(solution)/shard_map/convert_element_type | solution.py:241
  517.8 9.9 %fusion.71 = bf16[2,512,12,64]{1,3,2,0:T(8,128)(2,1)} fusion(bf16[2,12,512,512]{2,3,1,0:T(8,128)(2,1)} %multiply_convert_fusion.1, bf16[2,512,12,64]{1,0,3,2:T(2,128)(2,1)S(1)} %copy-done.10), kind=kOutput, calls=%fused_computation.159 | convolution fusion | flops 806879232 | bytes 15728640 | tf_op jit(solution)/shard_map/ihlm,ilhe->imhe/dot_general | solution.py:247
  527.7 6.7 fusion.70
  534.4 22.3 %fusion.141 = (f32[1024]{0:T(1024)S(1)}, f32[1024]{0:T(1024)S(1)}, f32[1024,768]{1,0:T(8,128)}) fusion(f32[1024]{0:T(1024)S(1)} %copy-done.70, f32[1024,768]{1,0:T(8,128)} %copy-done.37, f32[1024]{0:T(1024)S(1)} %copy-done.63, f32[768]{0:T(1024)S(1)} %get-tuple-element.63, f32[1024,768]{1,0:T(8,128)} %get-tuple-element.28, ...), kind=kOutput, calls=%fused_computation.258 | convolution fusion | flops 9717151744 | bytes 44071936 | tf_op jit(solution)/shard_map/tf,df->td/dot_general | solution.py:223
  556.8 5.8 convolution_convert_fusion.4
  566.7 12.6 %fusion.69 = bf16[2,512,12,64]{1,3,2,0:T(8,128)(2,1)} fusion(bf16[2,512,12,64]{1,0,3,2:T(2,128)(2,1)} %reshape.256, f32[2,12,512,512]{2,3,1,0:T(8,128)} %get-tuple-element.43, f32[2,12,512]{2,1,0:T(8,128)S(1)} %copy-done.45, pred[2,512]{1,0:T(4,128)(4,1)S(1)} %copy-done.53), kind=kOutput, calls=%fused_computation.157 | convolution fusion | flops 831258624 | bytes 28361728 | tf_op jit(solution)/shard_map/ihlm,ilhe->imhe/dot_general | solution.py:237
  579.3 21.5 %multiply_reduce_fusion = (f32[2,12,512]{2,1,0:T(8,128)S(1)}, f32[2,12,512,512]{2,3,1,0:T(8,128)}) fusion(f32[2,12,512,512]{2,3,1,0:T(8,128)} %get-tuple-element.43, f32[2,12,512]{2,1,0:T(8,128)S(1)} %copy-done.45, pred[2,512]{1,0:T(4,128)(4,1)S(1)} %copy-done.53, bf16[2,512,12,64]{1,0,3,2:T(2,128)(2,1)S(1)} %copy-done.29, bf16[2,512,12,64]{1,0,3,2:T(2,128)(2,1)} %reshape.256), kind=kOutput, calls=%fused_computation.1 | convolution fusion | flops 836751360 | bytes 53576704 | tf_op jit(solution)/shard_map/ilhe,imhe->ihlm/dot_general | solution.py:234
  600.8 22.0 %multiply_convert_fusion = bf16[2,12,512,512]{2,3,1,0:T(8,128)(2,1)} fusion(f32[2,12,512,512]{2,3,1,0:T(8,128)} %get-tuple-element.57, f32[2,12,512,512]{2,3,1,0:T(8,128)} %get-tuple-element.43, f32[2,12,512]{2,1,0:T(8,128)S(1)} %get-tuple-element.56, f32[2,12,512]{2,1,0:T(8,128)S(1)} %copy-done.45, pred[2,512]{1,0:T(4,128)(4,1)S(1)} %copy-done.53), kind=kLoop, calls=%fused_computation | loop fusion | flops 37748736 | bytes 63013888 | tf_op jit(solution)/shard_map/convert_element_type | solution.py:241
  622.9 9.8 %fusion.73 = bf16[2,512,12,64]{1,3,2,0:T(8,128)(2,1)} fusion(bf16[2,12,512,512]{2,3,1,0:T(8,128)(2,1)} %multiply_convert_fusion, bf16[2,512,12,64]{1,0,3,2:T(2,128)(2,1)S(1)} %copy-done.8), kind=kOutput, calls=%fused_computation.161 | convolution fusion | flops 806879232 | bytes 15728640 | tf_op jit(solution)/shard_map/ihlm,ilhe->imhe/dot_general | solution.py:247
  632.6 6.8 fusion.72
  642.2 3.8 stack_reshape.27
  651.4 2.8 stack_reshape.25
  658.5 4.6 fusion.105
  663.1 3.0 copy.240
  679.9 3.0 copy.255
  685.9 4.7 fusion.103
  693.2 38.5 %psum.7 = f32[2,8,768]{2,1,0:T(8,128)S(1)} all-reduce(f32[2,8,768]{2,1,0:T(8,128)S(1)} %fusion.101), channel_id=1, replica_groups=mesh['fsdp'=8,'rep'=4] {'fsdp','rep'}, use_global_device_ids=true, to_apply=%region_22.23 | all-reduce | flops 12288 | bytes 98304 | tf_op jit(solution)/shard_map/psum | solution.py:71
  736.4 8.4 %fusion.37 = bf16[1024,768]{1,0:T(8,128)(2,1)S(1)} fusion(f32[1024,768,1]{1,0,2:T(8,128)} %fusion.103, bf16[3,768,768]{2,1,0:T(8,128)(2,1)} %all-gather.9.cloned.1.call-done, bf16[1024,1,768]{2,0,1:T(8,128)(2,1)S(1)} %copy-done.26, bf16[1024,1,768]{2,0,1:T(8,128)(2,1)} %copy.242, bf16[1024,1,768]{2,0,1:T(8,128)(2,1)S(1)} %copy-done.27, ...), kind=kOutput, calls=%fused_computation.85 | convolution fusion | flops 3635675136 | bytes 19283968 | tf_op jit(solution)/shard_map/tke,kde->td/dot_general | solution.py:254
  744.9 6.3 fusion.36
  (284 shorter events, 100.0 us)
Async XLA Ops:
  7.2 136.5 %copy-start = (bf16[2,8,768]{2,1,0:T(8,128)(2,1)S(1)}, bf16[2,8,768]{2,1,0:T(8,128)(2,1)}, u32[]{:S(2)}) copy-start(bf16[2,8,768]{2,1,0:T(8,128)(2,1)} %param.20) | copy-start | bytes 73732
  7.2 70.5 %copy-start.86 = (u32[32]{0:T(128)S(1)}, u32[32]{0:T(128)}, u32[]{:S(2)}) copy-start(u32[32]{0:T(128)} %constant.158) | copy-start | bytes 388
  7.2 70.4 %copy-start.66 = (s32[4,2]{0,1:T(2,128)S(1)}, s32[4,2]{0,1:T(2,128)}, u32[]{:S(2)}) copy-start(s32[4,2]{0,1:T(2,128)} %param.15) | copy-start | bytes 100
  7.2 70.4 %copy-start.77 = (bf16[384]{0:T(512)(128)(2,1)S(1)}, bf16[384]{0:T(512)(128)(2,1)}, u32[]{:S(2)}) copy-start(bf16[384]{0:T(512)(128)(2,1)} %param.24) | copy-start | bytes 2308
  7.2 71.7 %copy-start.85 = (bf16[96]{0:T(256)(128)(2,1)S(1)}, bf16[96]{0:T(256)(128)(2,1)}, u32[]{:S(2)}) copy-start(bf16[96]{0:T(256)(128)(2,1)} %param.26) | copy-start | bytes 580
  7.2 84.5 %copy-start.78 = (bf16[2,96]{1,0:T(2,128)(2,1)S(1)}, bf16[2,96]{1,0:T(2,128)(2,1)}, u32[]{:S(2)}) copy-start(bf16[2,96]{1,0:T(2,128)(2,1)} %param.21) | copy-start | bytes 1156
  7.2 93.5 %copy-start.79 = (bf16[2,96]{1,0:T(2,128)(2,1)S(1)}, bf16[2,96]{1,0:T(2,128)(2,1)}, u32[]{:S(2)}) copy-start(bf16[2,96]{1,0:T(2,128)(2,1)} %param.22) | copy-start | bytes 1156
  7.2 101.4 %copy-start.76 = (bf16[3,96]{1,0:T(4,128)(2,1)S(1)}, bf16[3,96]{1,0:T(4,128)(2,1)}, u32[]{:S(2)}) copy-start(bf16[3,96]{1,0:T(4,128)(2,1)} %param.18) | copy-start | bytes 1732
  7.3 111.5 %copy-start.1 = (bf16[4,512,768]{2,1,0:T(8,128)(2,1)S(1)}, bf16[4,512,768]{2,1,0:T(8,128)(2,1)}, u32[]{:S(2)}) copy-start(bf16[4,512,768]{2,1,0:T(8,128)(2,1)} %param.27) | copy-start | bytes 9437188
  7.3 169.6 %all-gather.9.cloned.1.call-start = ((), (), s32[]{:S(2)}) async-start(), calls=%async_computation | async-start | bytes 3981312 | tf_op jit(solution)/shard_map/all_gather | solution.py:57
  7.3 10.1 %collective-permute-start = (bf16[3,96,192]{2,1,0:T(8,128)(2,1)}, bf16[3,96,192]{2,1,0:T(8,128)(2,1)S(1)}, u32[]{:S(2)}, u32[]{:S(2)}) collective-permute-start(bf16[3,96,192]{2,1,0:T(8,128)(2,1)} %param.16), channel_id=1, source_target_pairs={{0,1},{1,2},{2,3},{3,0},{4,5},{5,6},{6,7},{7,4},{8,9},{9,10},{10,1... | collective-permute-start | bytes 331784 | tf_op jit(solution)/shard_map/ppermute | solution.py:25
  10.4 11.7 %collective-permute-start.1 = (bf16[3,96,192]{2,1,0:T(8,128)(2,1)}, bf16[3,96,192]{2,1,0:T(8,128)(2,1)}, u32[]{:S(2)}, u32[]{:S(2)}) collective-permute-start(bf16[3,96,192]{2,1,0:T(8,128)(2,1)} %param.16), channel_id=1, source_target_pairs={{0,3},{1,0},{2,1},{3,2},{4,7},{5,4},{6,5},{7,6},{8,11},{9,8},{10,9... | collective-permute-start | bytes 331784 | tf_op jit(solution)/shard_map/ppermute | solution.py:30
  17.4 7.2 collective-permute-start.2
  26.4 250.0 %all-gather.11.cloned.1.call-start = ((), (), s32[]{:S(2)}) async-start(), calls=%async_computation.1 | async-start | bytes 1327104 | tf_op jit(solution)/shard_map/all_gather | solution.py:58
  44.0 84.6 %copy-start.75 = (bf16[2,96,8]{1,2,0:T(8,128)(2,1)S(1)}, bf16[2,96,8]{1,2,0:T(8,128)(2,1)}, u32[]{:S(2)}) copy-start(bf16[2,96,8]{1,2,0:T(8,128)(2,1)} %param.19) | copy-start | bytes 9220
  44.1 278.1 %all-gather.13.cloned.1.call-start = ((), (), s32[]{:S(2)}) async-start(), calls=%async_computation.2 | async-start | bytes 5308416 | tf_op jit(solution)/shard_map/all_gather | solution.py:59
  61.3 333.0 %all-gather.15.cloned.1.call-start = ((), (), s32[]{:S(2)}) async-start(), calls=%async_computation.3 | async-start | bytes 5308416 | tf_op jit(solution)/shard_map/all_gather | solution.py:60
  118.7 9.9 %copy-start.56 = (f32[768]{0:T(1024)}, f32[768]{0:T(1024)S(1)}, u32[]{:S(2)}) copy-start(f32[768]{0:T(1024)S(1)} %get-tuple-element.64) | copy-start | bytes 9220
  141.9 18.3 %copy-start.50 = (bf16[1024,2,8]{0,2,1:T(8,128)(2,1)}, bf16[1024,2,8]{0,2,1:T(8,128)(2,1)S(1)}, u32[]{:S(2)}) copy-start(bf16[1024,2,8]{0,2,1:T(8,128)(2,1)S(1)} %fusion.99) | copy-start | bytes 98308
  176.8 84.2 %copy-start.54 = (pred[2,512]{1,0:T(4,128)(4,1)}, pred[2,512]{1,0:T(4,128)(4,1)S(1)}, u32[]{:S(2)}) copy-start(pred[2,512]{1,0:T(4,128)(4,1)S(1)} %get-tuple-element.62) | copy-start | bytes 3076
  176.8 127.9 %copy-start.52 = (pred[2,512]{1,0:T(4,128)(4,1)}, pred[2,512]{1,0:T(4,128)(4,1)S(1)}, u32[]{:S(2)}) copy-start(pred[2,512]{1,0:T(4,128)(4,1)S(1)} %get-tuple-element.61) | copy-start | bytes 3076
  183.5 4.7 copy-start.81
  198.0 82.4 %copy-start.3 = (bf16[2,512,12,64]{1,0,3,2:T(2,128)(2,1)}, bf16[2,512,12,64]{1,0,3,2:T(2,128)(2,1)S(1)}, u32[]{:S(2)}) copy-start(bf16[2,512,12,64]{1,0,3,2:T(2,128)(2,1)S(1)} %convert_element_type.220) | copy-start | bytes 4718596
  212.8 19.7 %copy-start.5 = (bf16[2,512,12,64]{1,0,3,2:T(2,128)(2,1)}, bf16[2,512,12,64]{1,0,3,2:T(2,128)(2,1)S(1)}, u32[]{:S(2)}) copy-start(bf16[2,512,12,64]{1,0,3,2:T(2,128)(2,1)S(1)} %convert_element_type.205) | copy-start | bytes 4718596
  232.5 11.1 %copy-start.9 = (bf16[2,512,12,64]{1,0,3,2:T(2,128)(2,1)}, bf16[2,512,12,64]{1,0,3,2:T(2,128)(2,1)S(1)}, u32[]{:S(2)}) copy-start(bf16[2,512,12,64]{1,0,3,2:T(2,128)(2,1)S(1)} %get-tuple-element.36) | copy-start | bytes 4718596
  243.7 12.9 %copy-start.11 = (f32[2,512,12,64]{1,0,3,2:T(2,128)S(1)}, f32[2,512,12,64]{1,0,3,2:T(2,128)}, u32[]{:S(2)}) copy-start(f32[2,512,12,64]{1,0,3,2:T(2,128)} %mul.339) | copy-start | bytes 9437188
  243.7 12.9 %copy-start.12 = (f32[2,512,12,64]{1,0,3,2:T(2,128)S(1)}, f32[2,512,12,64]{1,0,3,2:T(2,128)}, u32[]{:S(2)}) copy-start(f32[2,512,12,64]{1,0,3,2:T(2,128)} %mul.359) | copy-start | bytes 9437188
  243.7 12.9 %copy-start.13 = (f32[2,512,12,64]{1,0,3,2:T(2,128)S(1)}, f32[2,512,12,64]{1,0,3,2:T(2,128)}, u32[]{:S(2)}) copy-start(f32[2,512,12,64]{1,0,3,2:T(2,128)} %squeeze.10) | copy-start | bytes 9437188
  243.7 12.9 %copy-start.14 = (f32[2,512,12,64]{1,0,3,2:T(2,128)S(1)}, f32[2,512,12,64]{1,0,3,2:T(2,128)}, u32[]{:S(2)}) copy-start(f32[2,512,12,64]{1,0,3,2:T(2,128)} %squeeze.8) | copy-start | bytes 9437188
  261.0 12.2 %copy-start.30 = (bf16[2,512,12,64]{1,0,3,2:T(2,128)(2,1)}, bf16[2,512,12,64]{1,0,3,2:T(2,128)(2,1)S(1)}, u32[]{:S(2)}) copy-start(bf16[2,512,12,64]{1,0,3,2:T(2,128)(2,1)S(1)} %get-tuple-element.38) | copy-start | bytes 4718596
  279.8 13.7 %copy-start.33 = (f32[1024,768]{1,0:T(8,128)}, f32[1024,768]{1,0:T(8,128)S(1)}, u32[]{:S(2)}) copy-start(f32[1024,768]{1,0:T(8,128)S(1)} %get-tuple-element.47) | copy-start | bytes 9437188
  279.8 175.0 %copy-start.59 = (f32[1024]{0:T(1024)}, f32[1024]{0:T(1024)S(1)}, u32[]{:S(2)}) copy-start(f32[1024]{0:T(1024)S(1)} %broadcast_multiply_fusion.10) | copy-start | bytes 12292
  280.3 174.5 %copy-start.67 = (f32[1024]{0:T(1024)}, f32[1024]{0:T(1024)S(1)}, u32[]{:S(2)}) copy-start(f32[1024]{0:T(1024)S(1)} %add_rsqrt_fusion.3) | copy-start | bytes 12292
  293.5 11.3 %copy-start.28 = (bf16[2,512,12,64]{1,0,3,2:T(2,128)(2,1)S(1)}, bf16[2,512,12,64]{1,0,3,2:T(2,128)(2,1)}, u32[]{:S(2)}) copy-start(bf16[2,512,12,64]{1,0,3,2:T(2,128)(2,1)} %get-tuple-element.39) | copy-start | bytes 4718596
  304.8 11.4 %copy-start.44 = (f32[2,12,512]{2,1,0:T(8,128)}, f32[2,12,512]{2,1,0:T(8,128)S(1)}, u32[]{:S(2)}) copy-start(f32[2,12,512]{2,1,0:T(8,128)S(1)} %log_add_fusion) | copy-start | bytes 147460
  319.9 10.5 %copy-start.62 = (f32[1024]{0:T(1024)}, f32[1024]{0:T(1024)S(1)}, u32[]{:S(2)}) copy-start(f32[1024]{0:T(1024)S(1)} %broadcast_multiply_fusion.8) | copy-start | bytes 12292
  322.1 8.4 %copy-start.69 = (f32[1024]{0:T(1024)}, f32[1024]{0:T(1024)S(1)}, u32[]{:S(2)}) copy-start(f32[1024]{0:T(1024)S(1)} %add_rsqrt_fusion.1) | copy-start | bytes 12292
  322.1 12.9 %copy-start.34 = (f32[1024,768]{1,0:T(8,128)S(1)}, f32[1024,768]{1,0:T(8,128)}, u32[]{:S(2)}) copy-start(f32[1024,768]{1,0:T(8,128)} %copy-done.33) | copy-start | bytes 9437188
  322.1 12.9 %copy-start.80 = (bf16[768,3072]{1,0:T(8,128)(2,1)S(1)}, bf16[768,3072]{1,0:T(8,128)(2,1)}, u32[]{:S(2)}) copy-start(bf16[768,3072]{1,0:T(8,128)(2,1)} %all-gather.13.cloned.1.call-done) | copy-start | bytes 14155780
  330.5 4.5 copy-start.87
  335.0 59.2 %copy-start.65 = (f32[768]{0:T(1024)S(1)}, f32[768]{0:T(1024)}, u32[]{:S(2)}) copy-start(f32[768]{0:T(1024)} %convert_element_type.214) | copy-start | bytes 9220
  432.6 22.8 %copy-start.35 = (f32[1024,768]{1,0:T(8,128)S(1)}, f32[1024,768]{1,0:T(8,128)}, u32[]{:S(2)}) copy-start(f32[1024,768]{1,0:T(8,128)} %copy-done.33) | copy-start | bytes 9437188
  463.7 12.7 %copy-start.31 = (bf16[2,512,12,64]{1,0,3,2:T(2,128)(2,1)S(1)}, bf16[2,512,12,64]{1,0,3,2:T(2,128)(2,1)}, u32[]{:S(2)}) copy-start(bf16[2,512,12,64]{1,0,3,2:T(2,128)(2,1)} %copy-done.30) | copy-start | bytes 4718596
  496.2 21.6 %copy-start.10 = (bf16[2,512,12,64]{1,0,3,2:T(2,128)(2,1)S(1)}, bf16[2,512,12,64]{1,0,3,2:T(2,128)(2,1)}, u32[]{:S(2)}) copy-start(bf16[2,512,12,64]{1,0,3,2:T(2,128)(2,1)} %copy-done.9) | copy-start | bytes 4718596
  517.8 9.9 %copy-start.6 = (bf16[2,512,12,64]{1,0,3,2:T(2,128)(2,1)S(1)}, bf16[2,512,12,64]{1,0,3,2:T(2,128)(2,1)}, u32[]{:S(2)}) copy-start(bf16[2,512,12,64]{1,0,3,2:T(2,128)(2,1)} %copy-done.5) | copy-start | bytes 4718596
  534.4 22.4 %copy-start.84 = (bf16[768,768]{1,0:T(8,128)(2,1)S(1)}, bf16[768,768]{1,0:T(8,128)(2,1)}, u32[]{:S(2)}) copy-start(bf16[768,768]{1,0:T(8,128)(2,1)} %all-gather.11.cloned.1.call-done) | copy-start | bytes 3538948
  566.7 12.6 %copy-start.29 = (bf16[2,512,12,64]{1,0,3,2:T(2,128)(2,1)S(1)}, bf16[2,512,12,64]{1,0,3,2:T(2,128)(2,1)}, u32[]{:S(2)}) copy-start(bf16[2,512,12,64]{1,0,3,2:T(2,128)(2,1)} %get-tuple-element.39) | copy-start | bytes 4718596
  600.8 22.0 %copy-start.8 = (bf16[2,512,12,64]{1,0,3,2:T(2,128)(2,1)S(1)}, bf16[2,512,12,64]{1,0,3,2:T(2,128)(2,1)}, u32[]{:S(2)}) copy-start(bf16[2,512,12,64]{1,0,3,2:T(2,128)(2,1)} %get-tuple-element.37) | copy-start | bytes 4718596
  622.8 9.8 %copy-start.4 = (bf16[2,512,12,64]{1,0,3,2:T(2,128)(2,1)S(1)}, bf16[2,512,12,64]{1,0,3,2:T(2,128)(2,1)}, u32[]{:S(2)}) copy-start(bf16[2,512,12,64]{1,0,3,2:T(2,128)(2,1)} %copy-done.3) | copy-start | bytes 4718596
  632.6 6.8 copy-start.41
  651.4 4.6 copy-start.51
  685.9 4.7 copy-start.49
  685.9 48.4 %copy-start.60 = (f32[1024]{0:T(1024)S(1)}, f32[1024]{0:T(1024)}, u32[]{:S(2)}) copy-start(f32[1024]{0:T(1024)} %copy-done.59) | copy-start | bytes 12292
  685.9 48.4 %copy-start.68 = (f32[1024]{0:T(1024)S(1)}, f32[1024]{0:T(1024)}, u32[]{:S(2)}) copy-start(f32[1024]{0:T(1024)} %copy-done.67) | copy-start | bytes 12292
  685.9 48.4 %copy-start.72 = (f32[1024]{0:T(1024)S(1)}, f32[1024]{0:T(1024)}, u32[]{:S(2)}) copy-start(f32[1024]{0:T(1024)} %copy-done.71) | copy-start | bytes 12292
  685.9 48.4 %copy-start.74 = (f32[1024]{0:T(1024)S(1)}, f32[1024]{0:T(1024)}, u32[]{:S(2)}) copy-start(f32[1024]{0:T(1024)} %copy-done.73) | copy-start | bytes 12292
  690.6 41.7 %copy-start.15 = (bf16[1024,768]{1,0:T(8,128)(2,1)S(1)}, bf16[1024,768]{1,0:T(8,128)(2,1)}, u32[]{:S(2)}) copy-start(bf16[1024,768]{1,0:T(8,128)(2,1)} %get-tuple-element.29) | copy-start | bytes 4718596
  690.6 41.7 %copy-start.16 = (bf16[1024,768]{1,0:T(8,128)(2,1)S(1)}, bf16[1024,768]{1,0:T(8,128)(2,1)}, u32[]{:S(2)}) copy-start(bf16[1024,768]{1,0:T(8,128)(2,1)} %get-tuple-element.30) | copy-start | bytes 4718596
  736.3 8.4 %copy-start.23 = (bf16[1024,1,768]{2,0,1:T(8,128)(2,1)S(1)}, bf16[1024,1,768]{2,0,1:T(8,128)(2,1)}, u32[]{:S(2)}) copy-start(bf16[1024,1,768]{2,0,1:T(8,128)(2,1)} %copy.261) | copy-start | bytes 4718596
  736.3 8.4 %copy-start.24 = (bf16[1024,1,768]{2,0,1:T(8,128)(2,1)S(1)}, bf16[1024,1,768]{2,0,1:T(8,128)(2,1)}, u32[]{:S(2)}) copy-start(bf16[1024,1,768]{2,0,1:T(8,128)(2,1)} %copy.259) | copy-start | bytes 4718596
  736.3 8.4 %copy-start.38 = (f32[1024,768]{1,0:T(8,128)S(1)}, f32[1024,768]{1,0:T(8,128)}, u32[]{:S(2)}) copy-start(f32[1024,768]{1,0:T(8,128)} %copy-done.37) | copy-start | bytes 9437188
  736.3 8.4 %copy-start.39 = (f32[1024,768,1]{1,0,2:T(8,128)S(1)}, f32[1024,768,1]{1,0,2:T(8,128)}, u32[]{:S(2)}) copy-start(f32[1024,768,1]{1,0,2:T(8,128)} %fusion.105) | copy-start | bytes 9437188
  736.3 8.4 %copy-start.40 = (bf16[1024,1,768]{2,0,1:T(8,128)(2,1)S(1)}, bf16[1024,1,768]{2,0,1:T(8,128)(2,1)}, u32[]{:S(2)}) copy-start(bf16[1024,1,768]{2,0,1:T(8,128)(2,1)} %copy.260) | copy-start | bytes 4718596
  736.3 8.5 %copy-start.82 = (bf16[3,768,768]{2,1,0:T(8,128)(2,1)S(1)}, bf16[3,768,768]{2,1,0:T(8,128)(2,1)}, u32[]{:S(2)}) copy-start(bf16[3,768,768]{2,1,0:T(8,128)(2,1)} %all-gather.9.cloned.1.call-done) | copy-start | bytes 10616836
  (31 other events, 72.0 us)
Sparse Core Ops, SparseCore 0:
  26.5 35.4 all-gather.8
  63.9 24.0 all-gather.10
  89.9 38.7 all-gather.12
  130.4 39.6 all-gather.14
